TPU v7x, 32 devices: a whole 2x2x4 slice. The times are simulated.
32 devices in a mesh: fsdp: 8 (over z, y), seq: 4 (over x, core).
Axes of the slice: x: 2, y: 2, z: 4, core: 2. Of those that a mesh axis runs over, the one named last changes fastest.
Arguments:
- inputs: bfloat16 [48, 512, 768], P('fsdp', 'seq'), may hold values from -6 to 6
- lengths: int32 [48], P('fsdp'), may hold values from 40 to 512, as said below
- w_query: bfloat16 [768, 768], P('fsdp'), may hold values from -0.3125 to 0.3125
- b_query: bfloat16 [768], P('fsdp'), may hold values from -3 to 3
- w_key: bfloat16 [768, 768], P('fsdp'), may hold values from -0.3125 to 0.3125
- w_value: bfloat16 [768, 768], P('fsdp'), may hold values from -0.21875 to 0.21875
- b_value: bfloat16 [768], P('fsdp'), may hold values from -3 to 3
- w_out: bfloat16 [768, 768], P('fsdp'), may hold values from -0.875 to 0.875
- b_out: bfloat16 [768], P('fsdp'), may hold values from -3 to 3
- gain_one: bfloat16 [768], P('fsdp'), may hold values from 0.5 to 1.5
- shift_one: bfloat16 [768], P('fsdp'), may hold values from -3 to 3
- w_inner: bfloat16 [768, 3072], P('fsdp'), may hold values from -0.21875 to 0.21875
- b_inner: bfloat16 [3072], P('fsdp'), may hold values from -3 to 3
- w_outer: bfloat16 [3072, 768], P('fsdp'), may hold values from -0.15625 to 0.15625
- b_outer: bfloat16 [768], P('fsdp'), may hold values from -3 to 3
- gain_two: bfloat16 [768], P('fsdp'), may hold values from 0.5 to 1.5
- shift_two: bfloat16 [768], P('fsdp'), may hold values from -3 to 3
- cotangent: bfloat16 [48, 512, 768], P('fsdp', 'seq'), may hold values from -6 to 6
Outputs:
- output: bfloat16 [48, 512, 768], P('fsdp', 'seq')
- grad_inputs: float32 [48, 512, 768], P('fsdp', 'seq')
- grad_w_query: float32 [768, 768], P('fsdp')
- grad_b_query: float32 [768], P('fsdp')
- grad_w_key: float32 [768, 768], P('fsdp')
- grad_w_value: float32 [768, 768], P('fsdp')
- grad_b_value: float32 [768], P('fsdp')
- grad_w_out: float32 [768, 768], P('fsdp')
- grad_b_out: float32 [768], P('fsdp')
- grad_gain_one: float32 [768], P('fsdp')
- grad_shift_one: float32 [768], P('fsdp')
- grad_w_inner: float32 [768, 3072], P('fsdp')
- grad_b_inner: float32 [3072], P('fsdp')
- grad_w_outer: float32 [3072, 768], P('fsdp')
- grad_b_outer: float32 [768], P('fsdp')
- grad_gain_two: float32 [768], P('fsdp')
- grad_shift_two: float32 [768], P('fsdp')
Inputs may be any that keep to these rules, and one draw needn't show every extreme that they name: `lengths`: real rows of each page; in every draw some page has exactly 512.
All inputs are finite; a program needn't handle non-finite values.
Results may differ from a plain program's by a relative error of at most 0.019.
Values may be sent and summed in bfloat16 or wider, within the bound.
A program may use at most 192 MiB of HBM per device.

v0:
```python
import functools
import math

import jax
import jax.numpy as jnp
from jax import lax
from jax.experimental import pallas as pl
from jax.experimental.pallas import tpu as pltpu
from jax.sharding import PartitionSpec as P

HEADS = 12
HEAD_DIM = 64
PAIR = 2 * HEAD_DIM
NEG = -1e30
EPS = 1e-12
BF = jnp.bfloat16
F32 = jnp.float32
MESH = pl.DeviceIdType.MESH
ANY = pl.BlockSpec(memory_space=pl.ANY)
VM = pl.BlockSpec(memory_space=pltpu.VMEM)
CHUNK = 1024
ROW = 96
VMEM_CAP = 60 << 20

NN = (((1,), (0,)), ((), ()))
NT = (((1,), (1,)), ((), ()))
TN = (((0,), (0,)), ((), ()))


def dot(a, b, dims=NN):
    return lax.dot_general(a, b, dims, preferred_element_type=F32)


def call(body, cost, **kw):
    flops, byts, trans = cost
    params = dict(vmem_limit_bytes=VMEM_CAP)
    params.update(kw.pop("params", {}))
    return pl.pallas_call(
        body,
        compiler_params=pltpu.CompilerParams(**params),
        cost_estimate=pl.CostEstimate(
            flops=int(flops), bytes_accessed=int(byts), transcendentals=int(trans)
        ),
        **kw,
    )


def attn_fwd_body(thr, xall, wq, wk, wv, vec, q_o, k_o, v_o, p_o, c_o, bias):
    page = pl.program_id(0)
    x_all = xall[0]
    own = x_all.shape[0] // 2
    query = (dot(x_all[:own], wq[...]) + vec[0:1, :]).astype(BF)
    q_o[0] = query
    k_o[0] = dot(x_all, wk[...]).astype(BF)
    v_o[0] = (dot(x_all, wv[...]) + vec[1:2, :]).astype(BF)
    blk = x_all.shape[0] // 4
    place = lax.broadcasted_iota(jnp.int32, (blk, own), 0)
    for b in range(4):
        bias[b * blk : (b + 1) * blk, :] = jnp.where(place < thr[page, b], 0.0, NEG)
    low_lane = lax.broadcasted_iota(jnp.int32, (own, PAIR), 1) < HEAD_DIM

    def pair(i, carry):
        cols = pl.ds(pl.multiple_of(i * PAIR, PAIR), PAIR)
        qp = q_o[0, :, cols] * jnp.array(1.0 / math.sqrt(HEAD_DIM), BF)
        kp = k_o[0, :, cols]
        vt = v_o[0, :, cols].T
        outs = []
        for h in range(2):
            keep = low_lane if h == 0 else jnp.logical_not(low_lane)
            qh = jnp.where(keep, qp, jnp.zeros_like(qp))
            st = dot(kp, qh, NT) + bias[...]
            top = jnp.max(st, axis=0, keepdims=True)
            ex = jnp.exp(st - top)
            tot = jnp.sum(ex, axis=0, keepdims=True)
            pt = (ex * (1.0 / tot)).astype(BF)
            p_o[0, 2 * i + h] = pt
            outs.append(dot(vt[h * HEAD_DIM : (h + 1) * HEAD_DIM], pt))
        c_o[0, :, cols] = jnp.concatenate(outs, axis=0).T.astype(BF)
        return carry

    lax.fori_loop(0, HEADS // 2, pair, 0)


def attn_fwd(thr, xall, wq, wk, wv, vec):
    pages, rows, d = xall.shape
    own = rows // 2
    const = lambda p, t: (0, 0)
    by_page = lambda p, t: (p, 0, 0)
    one = pl.Buffered(1)
    return call(
        attn_fwd_body,
        (
            pages * (2 * d * d * (own + 2 * rows) + 4 * own * rows * d),
            pages * rows * d * 2 * 4 + 6 * d * d + pages * HEADS * own * rows * 2,
            pages * HEADS * own * rows,
        ),
        grid_spec=pltpu.PrefetchScalarGridSpec(
            num_scalar_prefetch=1,
            grid=(pages,),
            in_specs=[pl.BlockSpec((1, rows, d), by_page)]
            + [pl.BlockSpec((d, d), const, pipeline_mode=one)] * 3
            + [pl.BlockSpec((8, d), const)],
            out_specs=[
                pl.BlockSpec((1, own, d), by_page),
                pl.BlockSpec((1, rows, d), by_page),
                pl.BlockSpec((1, rows, d), by_page),
                pl.BlockSpec((1, HEADS, rows, own), lambda p, t: (p, 0, 0, 0)),
                pl.BlockSpec((1, own, d), by_page),
            ],
            scratch_shapes=[pltpu.VMEM((rows, own), F32)],
        ),
        out_shape=[
            jax.ShapeDtypeStruct((pages, own, d), BF),
            jax.ShapeDtypeStruct((pages, rows, d), BF),
            jax.ShapeDtypeStruct((pages, rows, d), BF),
            jax.ShapeDtypeStruct((pages, HEADS, rows, own), BF),
            jax.ShapeDtypeStruct((pages, own, d), BF),
        ],
        name="attn_fwd",
    )(thr, xall, wq, wk, wv, vec)


def attn_bwd_body(q, k, v, p, ctx, dctx, dq_o, dk_own, dk_oth, dv_own, dv_oth):
    own = q.shape[1]
    low_lane = lax.broadcasted_iota(jnp.int32, (own, PAIR), 1) < HEAD_DIM
    scale = 1.0 / math.sqrt(HEAD_DIM)

    def pair(i, carry):
        cols = pl.ds(pl.multiple_of(i * PAIR, PAIR), PAIR)
        qp = q[0, :, cols] * jnp.array(scale, BF)
        kp = k[0, :, cols]
        kt = kp.T
        vp = v[0, :, cols]
        dc = dctx[0, :, cols]
        prod = (dc.astype(F32) * ctx[0, :, cols].astype(F32)).T
        dk = None
        dv = None
        dqs = []
        for h in range(2):
            keep = low_lane if h == 0 else jnp.logical_not(low_lane)
            feats = slice(h * HEAD_DIM, (h + 1) * HEAD_DIM)
            dch = jnp.where(keep, dc, jnp.zeros_like(dc))
            qh = jnp.where(keep, qp, jnp.zeros_like(qp))
            pt = p[0, 2 * i + h]
            delta = jnp.sum(prod[feats], axis=0, keepdims=True)
            dpt = dot(vp, dch, NT)
            dst = (pt.astype(F32) * (dpt - delta)).astype(BF)
            dvh = dot(pt, dch)
            dkh = dot(dst, qh)
            dk = dkh if dk is None else dk + dkh
            dv = dvh if dv is None else dv + dvh
            dqs.append(dot(kt[feats], dst))
        dq_o[0, :, cols] = (jnp.concatenate(dqs, axis=0) * scale).T.astype(BF)
        dk_own[0, :, cols] = dk[:own].astype(BF)
        dk_oth[0, :, cols] = dk[own:].astype(BF)
        dv_own[0, :, cols] = dv[:own].astype(BF)
        dv_oth[0, :, cols] = dv[own:].astype(BF)
        return carry

    lax.fori_loop(0, HEADS // 2, pair, 0)


def attn_bwd(q, k, v, p, ctx, dctx):
    pages, own, d = q.shape
    rows = k.shape[1]
    by_page = lambda i: (i, 0, 0)
    o = pl.BlockSpec((1, own, d), by_page)
    r = pl.BlockSpec((1, rows, d), by_page)
    return call(
        attn_bwd_body,
        (pages * 10 * own * rows * d, pages * (own * rows * HEADS * 2 + 10 * own * d * 2), 0),
        grid=(pages,),
        in_specs=[o, r, r, pl.BlockSpec((1, HEADS, rows, own), lambda i: (i, 0, 0, 0)), o, o],
        out_specs=[o] * 5,
        out_shape=[jax.ShapeDtypeStruct((pages, own, d), BF)] * 5,
        name="attn_bwd",
    )(q, k, v, p, ctx, dctx)


def normal_parts(v):
    bell = jnp.exp(v * v * -0.5)
    t = 1.0 / (1.0 + jnp.abs(v) * (0.3275911 / math.sqrt(2.0)))
    tail = t * (
        0.127414796 + t * (-0.142248368 + t * (0.7107068705 + t * (-0.7265760135 + t * 0.5307027145)))
    )
    tail = tail * bell
    return jnp.where(v >= 0.0, 1.0 - tail, tail), bell * (1.0 / math.sqrt(2.0 * math.pi))


def row_norm(v):
    centered = v - jnp.mean(v, -1, keepdims=True)
    inv = lax.rsqrt(jnp.mean(centered * centered, -1, keepdims=True) + EPS)
    return centered * inv, inv


def norm_back(e, n, inv):
    return inv * (e - jnp.mean(e, -1, keepdims=True) - n * jnp.mean(e * n, -1, keepdims=True))


def ffn_body(
    ctx, xall, cown, wo, wi_h, w2_h, vec, b_in,
    out, gm1_o, dctx_o, dwo_o, dwi_h, dw2_h, gvec, gbin,
    wi, w2, act, din, dgel, hid, gout, gatt, n1s, h1s, accs, r1s, dwi, dw2, lsem, osem,
):
    n, ff = act.shape
    pages, own, d = ctx.shape

    def cols_of(j):
        return pl.ds(pl.multiple_of(j * CHUNK, CHUNK), CHUNK)

    def loads(j):
        cols = cols_of(j)
        return (
            pltpu.make_async_copy(wi_h.at[:, cols], wi.at[:, cols], lsem.at[0, j]),
            pltpu.make_async_copy(w2_h.at[cols, :], w2.at[cols, :], lsem.at[1, j]),
        )

    def store_w2(j):
        return pltpu.make_async_copy(dw2.at[cols_of(j), :], dw2_h.at[cols_of(j), :], osem.at[0, j])

    def store_wi(j):
        return pltpu.make_async_copy(dwi.at[:, cols_of(j)], dwi_h.at[:, cols_of(j)], osem.at[1, j])

    n_chunks = ff // CHUNK
    for j in range(n_chunks):
        for copy in loads(j):
            copy.start()
    gvec[...] = jnp.zeros_like(gvec)

    def add(row, value):
        gvec[row : row + 1, :] += jnp.sum(value, 0, keepdims=True)

    for p in range(pages):
        r = slice(p * own, (p + 1) * own)
        mid = xall[p].astype(F32) + (dot(ctx[p], wo[...]) + vec[2:3, :])
        n1, r1 = row_norm(mid)
        n1s[r, :] = n1
        r1s[r, :] = jnp.broadcast_to(r1, (own, 128))
        h1 = n1 * vec[3:4, :] + vec[4:5, :]
        h1s[r, :] = h1
        hid[r, :] = h1.astype(BF)
    accs[...] = jnp.zeros_like(accs)

    def up(j, carry):
        cols = cols_of(j)
        for copy in loads(j):
            copy.wait()
        pre = dot(hid[...], wi[:, cols]) + b_in[:, cols]
        big, bell = normal_parts(pre)
        a = (pre * big).astype(BF)
        dgel[:, cols] = (big + pre * bell).astype(BF)
        act[:, cols] = a
        accs[...] += dot(a, w2[cols, :])
        return carry

    lax.fori_loop(0, n_chunks, up, 0)
    for p in range(pages):
        r = slice(p * own, (p + 1) * own)
        mid = h1s[r, :] + (accs[r, :] + vec[5:6, :])
        n2, r2 = row_norm(mid)
        out[p] = (n2 * vec[6:7, :] + vec[7:8, :]).astype(BF)
        cot = cown[p].astype(F32)
        gm2 = norm_back(cot * vec[6:7, :], n2, r2)
        go = gm2.astype(BF)
        gout[r, :] = go
        accs[r, :] = gm2
        add(5, go.astype(F32))
        add(6, cot * n2)
        add(7, cot)

    def down(j, carry):
        cols = cols_of(j)
        di = (dot(gout[...], w2[cols, :], NT) * dgel[:, cols].astype(F32)).astype(BF)
        din[:, cols] = di
        accs[...] += dot(di, wi[:, cols], NT)
        gbin[:, cols] = jnp.sum(di.astype(F32), 0, keepdims=True)
        dw2[cols, :] = dot(act[:, cols], gout[...], TN).astype(BF)
        store_w2(j).start()
        return carry

    lax.fori_loop(0, n_chunks, down, 0)
    for p in range(pages):
        r = slice(p * own, (p + 1) * own)
        gh = accs[r, :]
        n1 = n1s[r, :]
        gm1 = norm_back(gh * vec[3:4, :], n1, r1s[r, 0:1])
        gm1_o[p] = gm1
        ga = gm1.astype(BF)
        gatt[r, :] = ga
        dctx_o[p] = dot(ga, wo[...], NT).astype(BF)
        add(2, ga.astype(F32))
        add(3, gh * n1)
        add(4, gh)
    hid_t = hid[...].T

    def grads(j, carry):
        cols = cols_of(j)
        dwi[:, cols] = dot(hid_t, din[:, cols]).astype(BF)
        store_wi(j).start()
        return carry

    lax.fori_loop(0, n_chunks, grads, 0)
    dwo_o[...] = dot(ctx[...].reshape(n, d), gatt[...], TN).astype(BF)
    for j in range(n_chunks):
        store_w2(j).wait()
        store_wi(j).wait()


def ffn(ctx, xall, cown, wo, wi, w2, vec, b_in):
    pages, own, d = ctx.shape
    ff = wi.shape[1]
    n = pages * own
    sds = jax.ShapeDtypeStruct
    vm = pltpu.VMEM
    dma = pltpu.SemaphoreType.DMA
    return call(
        ffn_body,
        (n * d * (12 * ff + 6 * d), 4 * d * ff * 2 + 12 * n * d * 2, n * ff),
        grid=(1,),
        in_specs=[
            pl.BlockSpec((pages, own, d), lambda i: (0, 0, 0)),
            pl.BlockSpec((pages, own, d), lambda i: (0, 0, 0)),
            VM, VM, ANY, ANY, VM, VM,
        ],
        out_specs=[VM] * 4 + [ANY, ANY, VM, VM],
        out_shape=[
            sds((pages, own, d), BF), sds((pages, own, d), F32), sds((pages, own, d), BF),
            sds((d, d), BF), sds((d, ff), BF), sds((ff, d), BF), sds((8, d), F32), sds((1, ff), F32),
        ],
        scratch_shapes=[
            vm((d, ff), BF), vm((ff, d), BF), vm((n, ff), BF), vm((n, ff), BF), vm((n, ff), BF),
            vm((n, d), BF), vm((n, d), BF), vm((n, d), BF), vm((n, d), F32), vm((n, d), F32),
            vm((n, d), F32), vm((n, 128), F32), vm((d, ff), BF), vm((ff, d), BF),
            dma((2, ff // CHUNK)), dma((2, ff // CHUNK)),
        ],
        params=dict(vmem_limit_bytes=63 << 20),
        name="ffn",
    )(ctx, xall, cown, wo, wi, w2, vec, b_in)


def proj_body(
    xall, dq, dk, dkr, dv, dvr, gm1, wq, wk, wv,
    ga_o, gb_o, dwq_o, dwk_o, dwv_o, gvec, x_all, dq_all, dk_all, dv_all,
):
    page = pl.program_id(0)
    own = xall.shape[1]
    blk = own // 2
    here = pl.ds(pl.multiple_of(page * own, own), own)
    x_all[here, :] = xall[0]
    dq_v = dq[0]
    dk_v = (dk[0].astype(F32) + dkr[0].astype(F32)).astype(BF)
    dv_v = (dv[0].astype(F32) + dvr[0].astype(F32)).astype(BF)
    dq_all[here, :] = dq_v
    dk_all[here, :] = dk_v
    dv_all[here, :] = dv_v
    gx = gm1[0] + dot(dq_v, wq[...], NT) + dot(dk_v, wk[...], NT) + dot(dv_v, wv[...], NT)
    ga_o[0] = gx[:blk]
    gb_o[0] = gx[blk:].astype(BF)

    @pl.when(page == 0)
    def _():
        gvec[...] = jnp.zeros_like(gvec)

    gvec[0:1, :] += jnp.sum(dq_v.astype(F32), 0, keepdims=True)
    gvec[1:2, :] += jnp.sum(dv_v.astype(F32), 0, keepdims=True)

    @pl.when(page == pl.num_programs(0) - 1)
    def _():
        x_t = x_all[...].T
        dwq_o[...] = dot(x_t, dq_all[...]).astype(BF)
        dwk_o[...] = dot(x_t, dk_all[...]).astype(BF)
        dwv_o[...] = dot(x_t, dv_all[...]).astype(BF)


def proj(xall, dq, dk, dkr, dv, dvr, gm1, wq, wk, wv):
    pages, own, d = dq.shape
    blk = own // 2
    n = pages * own
    by_page = lambda p: (p, 0, 0)
    const = lambda p: (0, 0)
    one = pl.Buffered(1)
    half = pl.BlockSpec((1, blk, d), by_page)
    whole = pl.BlockSpec((1, own, d), by_page)
    square = pl.BlockSpec((d, d), const, pipeline_mode=one)
    return call(
        proj_body,
        (12 * n * d * d, 12 * d * d + 16 * n * d, 0),
        grid=(pages,),
        in_specs=[whole] * 7 + [square] * 3,
        out_specs=[half, half] + [square] * 3 + [pl.BlockSpec((8, d), const)],
        out_shape=[
            jax.ShapeDtypeStruct((pages, blk, d), F32),
            jax.ShapeDtypeStruct((pages, blk, d), BF),
        ]
        + [jax.ShapeDtypeStruct((d, d), BF)] * 3
        + [jax.ShapeDtypeStruct((8, d), F32)],
        scratch_shapes=[pltpu.VMEM((n, d), BF)] * 4,
        name="proj_bwd",
    )(xall, dq, dk, dkr, dv, dvr, gm1, wq, wk, wv)


def place():
    f, s = lax.axis_index("fsdp"), lax.axis_index("seq")
    return lax.div(f, 2), lax.rem(f, 2), lax.div(s, 2), lax.rem(s, 2)


def at(z, y, x, c):
    return {"fsdp": 2 * z + y, "seq": 2 * x + c}


def meet(others):
    barrier = pltpu.get_barrier_semaphore()
    for other in others:
        pl.semaphore_signal(barrier, inc=1, device_id=other, device_id_type=MESH)
    pl.semaphore_wait(barrier, len(others))


def remote(src, dst, send, recv, other):
    return pltpu.make_async_remote_copy(
        src_ref=src, dst_ref=dst, send_sem=send, recv_sem=recv,
        device_id=other, device_id_type=MESH,
    )


def begin(copy):
    copy.start()
    return copy


class Spread:
    def __init__(self, where, src, dst, row0, col0, width, sems, key, from0=None):
        self.z, self.y, self.x, self.c = where
        z, y, x, c = where
        zs, zr, fs, ys, yr, xs, xr, cs, cr, lo = sems
        k = key
        cols = pl.ds(pl.multiple_of(col0 + width * c, 128), width)
        origin = pl.ds(pl.multiple_of((col0 if from0 is None else from0) + width * c, 128), width)
        full = pl.ds(row0, ROW)
        mine = pl.ds(pl.multiple_of(row0 + (ROW - YROWS) * x, 16), YROWS)
        lacks = pl.ds(pl.multiple_of(row0 + YROWS * x, 16), ROW - YROWS)
        near, far, across = z + 1 - 2 * lax.rem(z, 2), lax.rem(z + 2, 4), 3 - z
        self.inner = jnp.logical_or(z == 1, z == 2)
        self.local = lambda: pltpu.make_async_copy(src.at[full, origin], dst.at[z, y, full, cols], lo.at[k])

        def send(block, n, target, sem):
            from_ref = src.at[full, origin] if block is None else dst.at[block, y, full, cols]
            b = z if block is None else block
            return remote(from_ref, dst.at[b, y, full, cols], sem, zr.at[k + (n,)], at(target, y, x, c))

        self.a = lambda: send(None, 0, near, zs.at[k + (0,)])
        self.b = lambda: send(None, 1, far, zs.at[k + (1,)])
        self.d = lambda: send(None, 2, across, zs.at[k + (2,)])
        self.fwd = lambda: send(far, 2, near, fs.at[k])
        yv = lambda: dst.at[:, y, mine, cols]
        self.ycopy = lambda: remote(yv(), yv(), ys.at[k], yr.at[k], at(z, 1 - y, x, c))
        xv = lambda: dst.at[:, 1 - y, lacks, cols]
        self.xcopy = lambda: remote(xv(), xv(), xs.at[k], xr.at[k], at(z, y, 1 - x, c))
        cv = lambda: dst.at[:, :, full, cols]
        self.ccopy = lambda: remote(cv(), cv(), cs.at[k], cr.at[k], at(z, y, x, 1 - c))

    def along_z(self):
        self.local().start()
        self.b().start()
        self.a().start()

        @pl.when(self.inner)
        def _():
            self.d().start()

    def forward(self):
        self.b().wait_recv()

        @pl.when(self.inner)
        def _():
            self.fwd().start()

    def along_y(self):
        self.a().wait_recv()
        self.d().wait_recv()
        self.local().wait()
        self.ycopy().start()

    def along_x(self):
        self.ycopy().wait_recv()
        self.xcopy().start()

    def to_core(self):
        self.xcopy().wait_recv()
        self.ccopy().start()

    def arrive(self):
        self.ccopy().wait_recv()

    def drain(self):
        self.a().wait_send()
        self.b().wait_send()

        @pl.when(self.inner)
        def _():
            self.d().wait_send()
            self.fwd().wait_send()

        self.ycopy().wait_send()
        self.xcopy().wait_send()
        self.ccopy().wait_send()


def spread_sems(*lead):
    dma = pltpu.SemaphoreType.DMA
    return [dma(lead + (3,)), dma(lead + (3,))] + [dma(lead)] * 8


GROUPS = 3
GCOLS = 256
REST = 9
EARLY = 3
YROWS = 64


def fwd_body(
    thr, x_in, cot, wq, wk, wv, wo, wi, w2, *refs,
):
    smalls = refs[:9]
    (
        gq_h, gk_h, gv_h, xall_h, q_h, k_h, v_h, c_h, p_o, dctx_h, gm1_h, dwo_h, dwi_h, dw2_h, fin_out, gvs, gbin,
    ) = refs[9:26]
    (
        gq, gk, gv, go, gi, g2, xall, q_o, k_o, v_o, c_o, cown, bias, pbuf, vpk, gvec, vec, b_in,
        act, dd, hid, gout, gatt, dctx, n1s, accs, r1s, dw2_s, dwi_s,
    ) = refs[26:55]
    qs, rs = refs[55:65], refs[65:75]
    asend, arecv, aloc, vs, vr, ps, outs_sem, grad_sem = refs[75:]
    z, y, x, c = where = place()
    f = 2 * z + y
    pages, rows = xall.shape[0], xall.shape[1]
    own, blk = rows // 2, rows // 4
    width = smalls[0].shape[-1]
    for i in range(8):
        vpk[i : i + 1, :width] = smalls[i][...].astype(F32).reshape(1, width)
    for i in range(3):
        vpk[8 + i : 9 + i, :] = smalls[8][:, 128 * i : 128 * (i + 1)].astype(F32).reshape(1, 128)
    gvec[f] = vpk[...]
    x_peer, c_peer = at(z, y, 1 - x, c), at(z, y, x, 1 - c)
    meet([{"fsdp": lax.rem(f + k + 1, 8)} for k in range(7)] + [x_peer, c_peer])

    groups = [
        [Spread(where, src, dst, 0, GCOLS * g, GCOLS // 2, qs, (g, w)) for w, (src, dst) in enumerate(((wq, gq), (wk, gk), (wv, gv)))]
        for g in range(GROUPS)
    ]

    def each(g, step):
        for part in groups[g]:
            getattr(part, step)()

    mine, sent = pl.ds(pages * x, pages), pl.ds(pages * (1 - x), pages)

    def band(b):
        return xall.at[:, pl.ds(blk * b, blk), :]

    to_b = remote(x_in.at[sent], band(1), asend.at[0], arecv.at[0], x_peer)
    to_c = remote(x_in.at[mine], band(2), asend.at[1], arecv.at[1], c_peer)
    to_d = remote(band(1), band(3), asend.at[2], arecv.at[2], c_peer)
    cot_b = remote(cot.at[sent], cown.at[:, pl.ds(blk, blk), :], asend.at[3], arecv.at[3], x_peer)
    keep_x = pltpu.make_async_copy(x_in.at[mine], band(0), aloc.at[0])
    keep_c = pltpu.make_async_copy(cot.at[mine], cown.at[:, pl.ds(0, blk), :], aloc.at[1])
    vecs = [
        remote(vpk, gvec.at[f], vs.at[k], vr.at[k], {"fsdp": lax.rem(f + k + 1, 8)}) for k in range(7)
    ]
    def rest(p, step):
        def run(src, dst, row0, col0, from0=None):
            getattr(Spread(where, src, dst, row0, col0, 384, rs, (p,), from0), step)()

        @pl.when(p == 0)
        def _():
            run(wo, go, 0, 0)

        @pl.when(jnp.logical_and(p >= 1, p < 5))
        def _():
            run(wi, gi.at[p - 1], 0, 0, 768 * (p - 1))

        @pl.when(jnp.logical_and(p >= 5, p < REST))
        def _():
            run(w2, g2, ROW * (p - 5), 0)

    to_b.start()
    each(0, "along_z")
    keep_x.start()
    to_c.start()
    for copy in vecs:
        copy.start()
    place_row = lax.broadcasted_iota(jnp.int32, (blk, own), 0)
    for page in range(pages):
        for b in range(4):
            bias[page, b * blk : (b + 1) * blk, :] = jnp.where(place_row < thr[page, b], 0.0, NEG)
    each(0, "forward")
    each(1, "along_z")
    each(0, "along_y")
    each(1, "forward")
    each(2, "along_z")
    each(1, "along_y")
    each(0, "along_x")
    each(2, "forward")
    for p in range(EARLY):
        rest(p, "along_z")
    each(2, "along_y")
    to_b.wait_recv()
    to_d.start()
    each(0, "to_core")
    each(1, "along_x")
    for copy in vecs:
        copy.wait_recv()
    for i in range(8):
        vec[i : i + 1, :] = jnp.concatenate([gvec[j, i : i + 1, :width] for j in range(8)], axis=1)
    for j in range(8):
        for i in range(3):
            b_in[:, (3 * j + i) * 128 : (3 * j + i + 1) * 128] = gvec[j, 8 + i : 9 + i, :]
    keep_c.start()
    keep_x.wait()
    to_c.wait_recv()
    to_d.wait_recv()
    each(0, "arrive")

    low_lane = lax.broadcasted_iota(jnp.int32, (own, PAIR), 1) < HEAD_DIM
    stages = (("along_z", 1 - 8 * EARLY // 3), ("forward", 0), ("along_y", 2), ("along_x", 5), ("to_core", 8))

    def tick(t):
        for step, late in stages:
            n = t - late
            p = lax.div(3 * n + 7, 8)

            @pl.when(jnp.logical_and(n >= 0, lax.div(8 * p, 3) == n))
            def _():
                if step == "along_z":
                    pl.when(p >= EARLY)(lambda: rest(p, step))
                else:
                    rest(p, step)

    def p_copy(page, pair, slot):
        return pltpu.make_async_copy(pbuf.at[slot], p_o.at[page, pl.ds(2 * pair, 2)], ps.at[slot])

    def unit(it, carry):
        g, page = lax.div(it, pages), lax.rem(it, pages)

        @pl.when(it == 0)
        def _():
            each(2, "along_x")
            each(1, "to_core")

        @pl.when(it == 1)
        def _():
            each(2, "to_core")
            cot_b.start()

        @pl.when(it == pages)
        def _():
            each(1, "arrive")

        @pl.when(it == 2 * pages)
        def _():
            each(2, "arrive")

        gcols = pl.ds(pl.multiple_of(g * GCOLS, GCOLS), GCOLS)
        x_all = xall[page]
        d = x_all.shape[1]
        query = (dot(x_all[:own], gq[:, :, :, gcols].reshape(d, GCOLS)) + vec[0:1, gcols]).astype(BF)
        keys = dot(x_all, gk[:, :, :, gcols].reshape(d, GCOLS)).astype(BF)
        vals = (dot(x_all, gv[:, :, :, gcols].reshape(d, GCOLS)) + vec[1:2, gcols]).astype(BF)
        q_o[page, :, gcols] = query
        k_o[page, :, gcols] = keys
        v_o[page, :, gcols] = vals
        for half in range(2):
            lanes = slice(half * PAIR, (half + 1) * PAIR)
            pair = 2 * g + half

            @pl.when(it > 0)
            def _():
                p_copy(page, pair, half).wait()

            qp = query[:, lanes] * jnp.array(1.0 / math.sqrt(HEAD_DIM), BF)
            kp = keys[:, lanes]
            vt = vals[:, lanes].T
            outs = []
            for h in range(2):
                keep = low_lane if h == 0 else jnp.logical_not(low_lane)
                qh = jnp.where(keep, qp, jnp.zeros_like(qp))
                st = dot(kp, qh, NT) + bias[page]
                top = jnp.max(st, axis=0, keepdims=True)
                ex = jnp.exp(st - top)
                tot = jnp.sum(ex, axis=0, keepdims=True)
                pt = (ex * (1.0 / tot)).astype(BF)
                pbuf[half, h] = pt
                outs.append(dot(vt[h * HEAD_DIM : (h + 1) * HEAD_DIM], pt))
            p_copy(page, pair, half).start()
            cols = pl.ds(pl.multiple_of(pair * PAIR, PAIR), PAIR)
            c_o[page, :, cols] = jnp.concatenate(outs, axis=0).T.astype(BF)
            tick(2 * it + half)
        return carry

    lax.fori_loop(0, GROUPS * pages, unit, 0)
    n_ticks = 2 * GROUPS * pages
    stores = [
        pltpu.make_async_copy(src, dst, outs_sem.at[i])
        for i, (src, dst) in enumerate(
            ((q_o, q_h), (k_o, k_h), (v_o, v_h), (c_o, c_h), (xall, xall_h), (gq, gq_h), (gk, gk_h), (gv, gv_h))
        )
    ]
    for copy in stores:
        copy.start()
    for half in range(2):
        p_copy(0, 0, half).wait()

    d = xall.shape[2]
    n_chunks = gi.shape[0]
    last = 8 * (REST - 1) // 3 + stages[-1][1] + 1
    gvs[...] = jnp.zeros_like(gvs)

    def add(row, value):
        gvs[row : row + 1, :] += jnp.sum(value, 0, keepdims=True)

    def square(ref):
        return ref[...].reshape(d, d)

    rest(0, "arrive")
    for page in range(pages):
        r = slice(page * own, (page + 1) * own)
        mid = xall[page, :own].astype(F32) + (dot(c_o[page], square(go)) + vec[2:3, :])
        n1, r1 = row_norm(mid)
        n1s[r, :] = n1
        r1s[r, :] = jnp.broadcast_to(r1, (own, 128))
        hid[r, :] = (n1 * vec[3:4, :] + vec[4:5, :]).astype(BF)

    def ticks(lo, hi):
        lax.fori_loop(lo, hi, lambda t, carry: (tick(t), carry)[1], 0)

    def up(j, carry):
        ticks(n_ticks + 3 * j, jnp.minimum(n_ticks + 3 * j + 3, last))
        rest(j + 1, "arrive")
        cols = pl.ds(pl.multiple_of(j * d, d), d)
        pre = dot(hid[...], gi[j].reshape(d, d)) + b_in[:, cols]
        big, bell = normal_parts(pre)
        act[:, cols] = (pre * big).astype(BF)
        dd[:, cols] = (big + pre * bell).astype(BF)
        return carry

    lax.fori_loop(0, n_chunks, up, 0)
    ticks(n_ticks + 3 * n_chunks, last)
    for p in range(5, REST):
        rest(p, "arrive")
    keep_c.wait()
    cot_b.wait_recv()
    stores[0].wait()

    def w2_rows(j):
        return g2[j].reshape(d, d)

    accs[...] = jnp.zeros_like(accs)

    def outer(j, carry):
        cols = pl.ds(pl.multiple_of(j * d, d), d)
        accs[...] += dot(act[:, cols], w2_rows(j))
        return carry

    lax.fori_loop(0, n_chunks, outer, 0)
    for page in range(pages):
        r = slice(page * own, (page + 1) * own)
        h1 = n1s[r, :] * vec[3:4, :] + vec[4:5, :]
        mid = h1 + (accs[r, :] + vec[5:6, :])
        n2, r2 = row_norm(mid)
        q_o[page] = (n2 * vec[6:7, :] + vec[7:8, :]).astype(BF)
        ct = cown[page].astype(F32)
        gm2 = norm_back(ct * vec[6:7, :], n2, r2)
        gob = gm2.astype(BF)
        gout[r, :] = gob
        accs[r, :] = gm2
        add(5, gob.astype(F32))
        add(6, ct * n2)
        add(7, ct)
    keep_out = pltpu.make_async_copy(q_o.at[:, pl.ds(0, blk), :], fin_out.at[mine], aloc.at[2])
    back_out = remote(q_o.at[:, pl.ds(blk, blk), :], fin_out.at[mine], asend.at[4], arecv.at[4], x_peer)
    keep_out.start()
    back_out.start()

    def grad_store(j, i):
        slot = lax.rem(j, 2)
        return pltpu.make_async_copy((dw2_s, dwi_s)[i].at[slot], (dw2_h, dwi_h)[i].at[j], grad_sem.at[i, slot])

    def down(j, carry):
        cols = pl.ds(pl.multiple_of(j * d, d), d)
        di = (dot(gout[...], w2_rows(j), NT) * dd[:, cols].astype(F32)).astype(BF)
        dd[:, cols] = di
        accs[...] += dot(di, gi[j].reshape(d, d), NT)
        gbin[:, cols] = jnp.sum(di.astype(F32), 0, keepdims=True)

        @pl.when(j >= 2)
        def _():
            grad_store(j, 0).wait()
            grad_store(j, 1).wait()

        slot = lax.rem(j, 2)
        dw2_s[slot] = dot(act[:, cols], gout[...], TN).astype(BF)
        dwi_s[slot] = dot(hid[...], di, TN).astype(BF)
        grad_store(j, 0).start()
        grad_store(j, 1).start()
        return carry

    lax.fori_loop(0, n_chunks, down, 0)
    for page in range(pages):
        r = slice(page * own, (page + 1) * own)
        gh = accs[r, :]
        n1 = n1s[r, :]
        gm1 = norm_back(gh * vec[3:4, :], n1, r1s[r, 0:1])
        accs[r, :] = gm1
        ga = gm1.astype(BF)
        gatt[r, :] = ga
        dctx[page] = dot(ga, square(go), NT).astype(BF)
        add(2, ga.astype(F32))
        add(3, gh * n1)
        add(4, gh)
    tail = [
        pltpu.make_async_copy(accs, gm1_h, outs_sem.at[8]),
        pltpu.make_async_copy(dctx, dctx_h, outs_sem.at[9]),
        pltpu.make_async_copy(hid, dwo_h, outs_sem.at[10]),
    ]
    tail[0].start()
    tail[1].start()
    hid[...] = dot(c_o[...].reshape(pages * own, d), gatt[...], TN).astype(BF)
    tail[2].start()
    for j in range(n_chunks - 2, n_chunks):
        grad_store(j, 0).wait()
        grad_store(j, 1).wait()

    def finish(p, carry):
        rest(p, "drain")
        return carry

    lax.fori_loop(0, REST, finish, 0)
    for g in range(GROUPS):
        each(g, "drain")
    for copy in vecs + [to_b, to_c, to_d, cot_b]:
        copy.wait_send()
    for copy in stores[1:] + tail + [keep_out]:
        copy.wait()
    back_out.wait()


def fwd(thr, x_in, cot, ws, smalls):
    pages_all, blk, d = x_in.shape
    pages, own, rows = pages_all // 2, 2 * blk, 4 * blk
    n = pages * own
    dma = pltpu.SemaphoreType.DMA
    sds = jax.ShapeDtypeStruct
    vm = pltpu.VMEM
    ff = ws[4].shape[1]
    quarter = (4, 2, ROW, d)
    res = call(
        fwd_body,
        (n * d * (12 * ff + 12 * d), sum(16 * w.size for w in ws), pages * HEADS * own * rows),
        in_specs=[pl.BlockSpec(memory_space=pltpu.SMEM)] + [ANY] * 5 + [VM] * 12,
        out_specs=[ANY] * 15 + [VM, VM],
        out_shape=[sds(quarter, BF)] * 3
        + [
            sds((pages, rows, d), BF),
            sds((pages, own, d), BF), sds((pages, rows, d), BF), sds((pages, rows, d), BF), sds((pages, own, d), BF),
            sds((pages, HEADS, rows, own), BF),
            sds((pages, own, d), BF), sds((n, d), F32), sds((d, d), BF),
            sds((ff // d, d, d), BF), sds((ff // d, d, d), BF), sds((pages_all, blk, d), BF),
            sds((8, d), F32), sds((1, ff), F32),
        ],
        scratch_shapes=[
            vm(quarter, BF), vm(quarter, BF), vm(quarter, BF), vm(quarter, BF),
            vm((ff // d,) + quarter, BF), vm((4, 2, ff // 8, d), BF),
            vm((pages, rows, d), BF), vm((pages, own, d), BF), vm((pages, rows, d), BF), vm((pages, rows, d), BF),
            vm((pages, own, d), BF), vm((pages, own, d), BF), vm((pages, rows, own), F32), vm((2, 2, rows, own), BF),
            vm((16, 128), F32), vm((8, 16, 128), F32), vm((8, d), F32), vm((1, ff), F32),
            vm((n, ff), BF), vm((n, ff), BF), vm((n, d), BF), vm((n, d), BF), vm((n, d), BF), vm((pages, own, d), BF),
            vm((n, d), F32), vm((n, d), F32), vm((n, 128), F32), vm((2, d, d), BF), vm((2, d, d), BF),
        ]
        + spread_sems(GROUPS, 3)
        + spread_sems(REST)
        + [dma((5,)), dma((5,)), dma((3,)), dma((7,)), dma((7,)), dma((2,)), dma((11,)), dma((2, 2))],
        params=dict(collective_id=0, has_side_effects=True, vmem_limit_bytes=64 << 20),
        name="gather_forward",
    )(thr, x_in, cot, *ws, *smalls)
    full = [r.reshape(d, d) for r in res[:3]]
    return full, res[3:]


class Fold:
    def __init__(self, where, acc, bufs, sems, key, keep):
        self.z, self.y, self.x, self.c = where
        self.acc, self.key = acc, key
        give = ROW - keep
        self.rc, self.rx, self.ry, self.rz, self.fin, self.rf = [b.at[key] for b in bufs]
        self.cs, self.cr, self.xs, self.xr, self.ys, self.yr, self.zs, self.zr, self.fs, self.fr, self.es, self.er = sems
        z = self.z
        self.near, self.far, self.across = z + 1 - 2 * lax.rem(z, 2), lax.rem(z + 2, 4), 3 - z
        self.inner = jnp.logical_or(z == 1, z == 2)
        self.outer = jnp.logical_not(self.inner)
        self.keep = pl.ds(pl.multiple_of(give * self.x, 16), keep)
        self.give = pl.ds(pl.multiple_of(keep * (1 - self.x), 16), give)
        self.gain = pl.ds(pl.multiple_of(keep * self.x, 16), give)

    def part(self, *sel):
        return self.acc(sel)

    def xcopy(self):
        return remote(
            self.part(ALL, 1 - self.y, self.give), self.rx, self.xs.at[self.key], self.xr.at[self.key],
            at(self.z, self.y, 1 - self.x, self.c),
        )

    def ycopy(self):
        return remote(
            self.part(ALL, 1 - self.y, self.keep), self.ry, self.ys.at[self.key], self.yr.at[self.key],
            at(self.z, 1 - self.y, self.x, self.c),
        )

    def zcopy(self, block, target, slot):
        return remote(
            self.part(block, self.y, ALL), self.rz.at[slot], self.zs.at[self.key + (slot,)],
            self.zr.at[self.key + (slot,)], at(target, self.y, self.x, self.c),
        )

    def a(self):
        return self.zcopy(self.near, self.near, 0)

    def b(self):
        return self.zcopy(self.far, self.far, 1)

    def d(self):
        return self.zcopy(self.across, self.across, 2)

    def f(self):
        return self.zcopy(self.across, self.near, 3)

    def fcopy(self):
        return remote(
            self.fin, self.rf, self.fs.at[self.key], self.fr.at[self.key],
            at(self.z, self.y, 1 - self.x, self.c),
        )

    def over_x(self, first):
        first.wait_recv()
        whole = self.part(ALL, ALL, ALL)
        whole[...] = whole[...] + self.rc[...]
        self.xcopy().start()

    def over_y(self):
        self.xcopy().wait_recv()
        rows = self.part(ALL, 1 - self.y, self.gain)
        rows[...] = rows[...] + self.rx[...]
        self.ycopy().start()

    def over_z(self):
        self.ycopy().wait_recv()
        rows = self.part(ALL, self.y, self.keep)
        rows[...] = rows[...] + self.ry[...]
        self.a().start()

        @pl.when(self.outer)
        def _():
            self.f().start()
            self.b().start()

        @pl.when(self.inner)
        def _():
            self.d().start()

    def inside(self):
        @pl.when(self.inner)
        def _():
            self.f().wait_recv()
            rows = self.part(self.far, self.y, ALL)
            rows[...] = rows[...] + self.rz[3]
            self.b().start()

    def total(self):
        self.a().wait_recv()
        self.b().wait_recv()
        own = self.part(self.z, self.y, ALL)

        @pl.when(self.outer)
        def _():
            self.fin[...] = (own[...].astype(F32) + self.rz[0].astype(F32) + self.rz[1].astype(F32)).astype(BF)

        @pl.when(self.inner)
        def _():
            self.d().wait_recv()
            self.fin[...] = (
                own[...].astype(F32) + self.rz[0].astype(F32) + self.rz[1].astype(F32) + self.rz[2].astype(F32)
            ).astype(BF)

        self.fcopy().start()

    def ecopy(self, view):
        return remote(view, view, self.es.at[self.key], self.er.at[self.key], at(self.z, self.y, self.x, 1 - self.c))

    def write(self, view):
        self.fcopy().wait_recv()
        view[...] = self.fin[...].astype(F32) + self.rf[...].astype(F32)
        self.ecopy(view).start()

    def drain(self, first, view):
        self.ecopy(view).wait_recv()
        first.wait_send()
        self.xcopy().wait_send()
        self.ycopy().wait_send()
        self.a().wait_send()
        self.b().wait_send()

        @pl.when(self.outer)
        def _():
            self.f().wait_send()

        @pl.when(self.inner)
        def _():
            self.d().wait_send()

        self.fcopy().wait_send()
        self.ecopy(view).wait_send()


ALL = slice(None)
KEEP_REST = 64
KEEP_GROUP = 80


def fold_sems(*lead):
    dma = pltpu.SemaphoreType.DMA
    return [dma(lead)] * 6 + [dma(lead + (4,))] * 2 + [dma(lead)] * 4


def fold_bufs(width, keep, *lead):
    return [
        pltpu.VMEM(lead + shape, BF)
        for shape in (
            (4, 2, ROW, width), (4, ROW - keep, width), (4, keep, width), (4, ROW, width), (ROW, width), (ROW, width),
        )
    ]


def bwd_body(
    q_h, k_h, v_h, c_h, dc_h, g1_h, x_h, gq_h, gk_h, gv_h, p_h, dwo, dwi, dw2, gvf, gbin,
    oq, ok, ov, oo, oi, o2, gx, ovec,
    *refs,
):
    q_v, k_v, v_v, c_v, dc_v, g1_v, x_v, gq_v, gk_v, gv_v = refs[:10]
    (acc, dwg, dq_all, dk_all, dv_all, rk, rv, sk, sv, pbuf, x_t, gxs, rgx, pack, vecin, vtot, vx, brow) = refs[10:28]
    fb, gb = refs[28:34], refs[34:40]
    fsem, gsem = refs[40:52], refs[52:64]
    lsem, csem, ps, ks, kr, gs, gr, vs, vr, us, ur = refs[64:]
    z, y, x, c = where = place()
    f = 2 * z + y
    pages, own, d = q_h.shape
    blk = own // 2
    rows = k_h.shape[1]
    x_peer, c_peer = at(z, y, 1 - x, c), at(z, y, x, 1 - c)
    meet([{"fsdp": lax.rem(f + k + 1, 8)} for k in range(7)] + [x_peer, c_peer])

    def first_of(p):
        def run(src, row0, col0, go):
            rr = pl.ds(row0, ROW)
            mine = src.at[:, :, rr, pl.ds(pl.multiple_of(col0 + 384 * c, 128), 384)]
            other = src.at[:, :, rr, pl.ds(pl.multiple_of(col0 + 384 * (1 - c), 128), 384)]
            copy = pltpu.make_async_copy(mine, acc.at[p], csem.at[p])
            send = remote(other, fb[0].at[p], fsem[0].at[p], fsem[1].at[p], c_peer)
            if go:
                copy.start()
                send.start()
            return copy, send

        return run

    def rest_src(p, run):
        @pl.when(p < 4)
        def _():
            run(dw2, ROW * p, 0)

        @pl.when(jnp.logical_and(p >= 4, p < 8))
        def _():
            run(dwi.at[p - 4], 0, 0)

        @pl.when(p == 8)
        def _():
            run(dwo, 0, 0)

    def rest_out(p, run):
        @pl.when(p < 4)
        def _():
            run(o2.at[pl.ds(pl.multiple_of(ROW * p, 32), ROW), pl.ds(pl.multiple_of(384 * c, 128), 384)])

        @pl.when(jnp.logical_and(p >= 4, p < 8))
        def _():
            run(oi.at[:, pl.ds(pl.multiple_of(768 * (p - 4) + 384 * c, 128), 384)])

        @pl.when(p == 8)
        def _():
            run(oo.at[:, pl.ds(pl.multiple_of(384 * c, 128), 384)])

    def fold(p):
        return Fold(where, lambda sel: acc.at[(p,) + sel], fb, fsem, (p,), KEEP_REST)

    def any_first(p):
        return remote(fb[0].at[p], fb[0].at[p], fsem[0].at[p], fsem[1].at[p], c_peer)

    def step(p, name):
        ok_p = jnp.logical_and(p >= 0, p < REST)

        @pl.when(ok_p)
        def _():
            if name == "start":
                rest_src(p, lambda src, r0, c0: first_of(p)(src, r0, c0, True) and None)
            elif name == "over_x":
                pltpu.make_async_copy(acc.at[p], acc.at[p], csem.at[p]).wait()
                fold(p).over_x(any_first(p))
            elif name == "write":
                rest_out(p, lambda view: fold(p).write(view))
            elif name == "drain":
                rest_out(p, lambda view: fold(p).drain(any_first(p), view))
            else:
                getattr(fold(p), name)()

    def gfold(g, w):
        cols = pl.ds(pl.multiple_of(128 * c, 128), 128)
        return Fold(where, lambda sel: dwg.at[(g, w) + sel + (cols,)], gb, gsem, (g, w), KEEP_GROUP)

    def gfirst(g, w):
        cols = pl.ds(pl.multiple_of(128 * (1 - c), 128), 128)
        return remote(dwg.at[g, w, :, :, :, cols], gb[0].at[g, w], gsem[0].at[g, w], gsem[1].at[g, w], c_peer)

    def gstep(g, name):
        for w, o in enumerate((oq, ok, ov)):
            view = o.at[:, pl.ds(pl.multiple_of(GCOLS * g + 128 * c, 128), 128)]
            if name == "start":
                gfirst(g, w).start()
            elif name == "over_x":
                gfold(g, w).over_x(gfirst(g, w))
            elif name == "write":
                gfold(g, w).write(view)
            elif name == "drain":
                gfold(g, w).drain(gfirst(g, w), view)
            else:
                getattr(gfold(g, w), name)()

    stages = (("over_x", 0), ("over_y", 6), ("over_z", 14), ("inside", 19), ("total", 23), ("write", 28))
    pace = 3
    last = pace * (REST + GROUPS - 1) + stages[-1][1] + 1

    def tick(t):
        for name, late in stages:
            n = t - late
            p = lax.div(n, pace)

            @pl.when(jnp.logical_and(n >= 0, jnp.logical_and(lax.rem(n, pace) == 0, p < REST + GROUPS)))
            def _():
                step(p, name)

                @pl.when(p >= REST)
                def _():
                    gstep(p - REST, name)

    loads = [
        pltpu.make_async_copy(src, dst, lsem.at[i])
        for i, (src, dst) in enumerate(
            (
                (q_h, q_v), (k_h, k_v), (v_h, v_v), (c_h, c_v), (dc_h, dc_v), (x_h.at[:, pl.ds(0, own), :], x_v),
                (g1_h, g1_v), (gq_h, gq_v), (gk_h, gk_v), (gv_h, gv_v),
            )
        )
    ]

    def p_copy(it, half):
        g, page = lax.div(it, pages), lax.rem(it, pages)
        return pltpu.make_async_copy(p_h.at[page, pl.ds(4 * g + 2 * half, 2)], pbuf.at[half], ps.at[half])

    for half in range(2):
        p_copy(0, half).start()
    for copy in loads[:5]:
        copy.start()
    for p in range(REST):
        step(p, "start")
    for copy in loads[5:]:
        copy.start()
    for copy in loads[:5]:
        copy.wait()

    low_lane = lax.broadcasted_iota(jnp.int32, (own, PAIR), 1) < HEAD_DIM
    scale = 1.0 / math.sqrt(HEAD_DIM)

    def kv_send(it):
        g, page = lax.div(it, pages), lax.rem(it, pages)
        gcols = pl.ds(pl.multiple_of(g * GCOLS, GCOLS), GCOLS)
        return [
            remote(s_ref.at[page, :, gcols], r_ref.at[page, :, gcols], ks.at[g, page, i], kr.at[g, page, i], c_peer)
            for i, (s_ref, r_ref) in enumerate(((sk, rk), (sv, rv)))
        ]

    def attend(it, half):
        g, page = lax.div(it, pages), lax.rem(it, pages)
        here = pl.ds(pl.multiple_of(page * own, own), own)
        p_copy(it, half).wait()
        cols = pl.ds(pl.multiple_of(g * GCOLS + half * PAIR, PAIR), PAIR)
        qp = q_v[page, :, cols] * jnp.array(scale, BF)
        kp = k_v[page, :, cols]
        kt = kp.T
        vp = v_v[page, :, cols]
        dc = dc_v[page, :, cols]
        prod = (dc.astype(F32) * c_v[page, :, cols].astype(F32)).T
        dk = None
        dv = None
        dqs = []
        for h in range(2):
            keep = low_lane if h == 0 else jnp.logical_not(low_lane)
            feats = slice(h * HEAD_DIM, (h + 1) * HEAD_DIM)
            dch = jnp.where(keep, dc, jnp.zeros_like(dc))
            qh = jnp.where(keep, qp, jnp.zeros_like(qp))
            pt = pbuf[half, h]
            delta = jnp.sum(prod[feats], axis=0, keepdims=True)
            dpt = dot(vp, dch, NT)
            dst = (pt.astype(F32) * (dpt - delta)).astype(BF)
            dvh = dot(pt, dch)
            dkh = dot(dst, qh)
            dk = dkh if dk is None else dk + dkh
            dv = dvh if dv is None else dv + dvh
            dqs.append(dot(kt[feats], dst))
        dq_all[here, cols] = (jnp.concatenate(dqs, axis=0) * scale).T.astype(BF)
        dk_all[here, cols] = dk[:own].astype(BF)
        sk[page, :, cols] = dk[own:].astype(BF)
        dv_all[here, cols] = dv[:own].astype(BF)
        sv[page, :, cols] = dv[own:].astype(BF)

        @pl.when(it + 1 < GROUPS * pages)
        def _():
            p_copy(it + 1, half).start()

    def group_grads(g):
        gcols = pl.ds(pl.multiple_of(g * GCOLS, GCOLS), GCOLS)
        for page in range(pages):
            here = pl.ds(page * own, own)
            for copy in kv_send(g * pages + page):
                copy.wait_recv()
            dk_all[here, gcols] = dk_all[here, gcols] + rk[page, :, gcols]
            dv_all[here, gcols] = dv_all[here, gcols] + rv[page, :, gcols]
        for w, grad in enumerate((dq_all, dk_all, dv_all)):
            value = grad[:, gcols]
            dwg[g, w] = dot(x_t[...], value).astype(BF).reshape(4, 2, ROW, GCOLS)
            if w != 1:
                brow[w : w + 1, gcols] = jnp.sum(value.astype(F32), 0, keepdims=True)
        gstep(g, "start")

    def gx_send(page):
        return remote(gxs.at[page], rgx.at[page], gs.at[page], gr.at[page], x_peer)

    def input_grads(page):
        here = pl.ds(pl.multiple_of(page * own, own), own)
        total = g1_v[page]
        for grad, w in ((dq_all, gq_v), (dk_all, gk_v), (dv_all, gv_v)):
            total = total + dot(grad[here, :], w[...], NT)
        gx[pages * x + page] = total[:blk]
        gxs[page] = total[blk:].astype(BF)
        gx_send(page).start()

    n_it = GROUPS * pages

    def unit(it, carry):
        for half in range(2):

            @pl.when(it < n_it)
            def _():
                attend(it, half)

            if half == 1:

                @pl.when(it < n_it)
                def _():
                    for copy in kv_send(it):
                        copy.start()

            tick(2 * it + half)

        @pl.when(it == 0)
        def _():
            for copy in loads[5:]:
                copy.wait()
            x_t[...] = x_v[...].reshape(pages * own, d).T

        @pl.when(jnp.logical_and(it > 0, jnp.logical_and(lax.rem(it, pages) == 0, it <= n_it)))
        def _():
            group_grads(lax.div(it, pages) - 1)

        page = it - n_it

        @pl.when(jnp.logical_and(page >= 0, page < pages))
        def _():
            input_grads(page)

        return carry

    def vec_send(k):
        to = lax.rem(f + k + 1, 8)
        return remote(pack.at[to], vecin.at[k], vs.at[k], vr.at[k], {"fsdp": to})

    vec_x = lambda: remote(vtot, vx.at[0], us.at[0], ur.at[0], x_peer)
    vec_c = lambda: remote(vx.at[1], vx.at[2], us.at[1], ur.at[1], c_peer)

    def small_pack():
        for i in range(8):
            row = brow[0:1, :] if i == 0 else brow[2:3, :] if i == 1 else gvf[i : i + 1, :]
            for j in range(8):
                pack[j, i : i + 1, :ROW] = row[:, ROW * j : ROW * (j + 1)]
        for j in range(8):
            for i in range(3):
                pack[j, 8 + i : 9 + i, :] = gbin[:, (3 * j + i) * 128 : (3 * j + i + 1) * 128]
        for k in range(7):
            vec_send(k).start()

    def small_sum():
        total = pack[f]
        for k in range(7):
            vec_send(k).wait_recv()
            total = total + vecin[k]
        vtot[...] = total
        vec_x().start()

    def small_pair():
        vec_x().wait_recv()
        vx[1] = vtot[...] + vx[0]
        vec_c().start()

    def all_steps(it, carry):
        unit(it, carry)
        for when, run in ((n_it, small_pack), (n_it + 3, small_sum), (n_it + 6, small_pair)):
            pl.when(it == when)(run)
        return carry

    lax.fori_loop(0, (last + 1) // 2, all_steps, 0)
    for page in range(pages):
        gx_send(page).wait_recv()
        gx[pages * (1 - x) + page] = rgx[page].astype(F32)
    vec_c().wait_recv()
    ovec[...] = vx[1] + vx[2]

    def finish(p, carry):
        step(p, "drain")
        return carry

    lax.fori_loop(0, REST, finish, 0)
    for g in range(GROUPS):
        gstep(g, "drain")
    for it in range(n_it):
        for copy in kv_send(it):
            copy.wait_send()
    for page in range(pages):
        gx_send(page).wait_send()
    for k in range(7):
        vec_send(k).wait_send()
    vec_x().wait_send()
    vec_c().wait_send()


def bwd(q, k, v, ctx, dctx, gm1, xall, ws, p, grads, gvf, gbin, shards):
    pages, own, d = q.shape
    rows, blk = k.shape[1], own // 2
    n = pages * own
    dma = pltpu.SemaphoreType.DMA
    vm = pltpu.VMEM
    sds = jax.ShapeDtypeStruct
    dwo, dwi, dw2 = grads
    views = [dwo.reshape(4, 2, ROW, d), dwi.reshape(-1, 4, 2, ROW, d), dw2.reshape((4, 2) + shards[5])]
    res = call(
        bwd_body,
        (12 * n * d * d + pages * 10 * own * rows * d, sum(16 * g.size for g in grads), 0),
        in_specs=[ANY] * 14 + [VM, VM],
        out_specs=[VM] * 8,
        out_shape=[sds(shape, F32) for shape in shards]
        + [sds((2 * pages, blk, d), F32), sds((16, 128), F32)],
        scratch_shapes=[
            vm((pages, own, d), BF), vm((pages, rows, d), BF), vm((pages, rows, d), BF),
            vm((pages, own, d), BF), vm((pages, own, d), BF), vm((pages, own, d), F32), vm((pages, own, d), BF),
            vm((d, d), BF), vm((d, d), BF), vm((d, d), BF),
            vm((REST, 4, 2, ROW, 384), BF), vm((GROUPS, 3, 4, 2, ROW, GCOLS), BF),
            vm((n, d), BF), vm((n, d), BF), vm((n, d), BF),
            vm((pages, own, d), BF), vm((pages, own, d), BF), vm((pages, own, d), BF), vm((pages, own, d), BF),
            vm((2, 2, rows, own), BF), vm((d, n), BF), vm((pages, blk, d), BF), vm((pages, blk, d), BF),
            vm((8, 16, 128), F32), vm((7, 16, 128), F32), vm((16, 128), F32), vm((3, 16, 128), F32), vm((8, d), F32),
        ]
        + fold_bufs(384, KEEP_REST, REST)
        + fold_bufs(128, KEEP_GROUP, GROUPS, 3)
        + fold_sems(REST)
        + fold_sems(GROUPS, 3)
        + [
            dma((10,)), dma((REST,)), dma((2,)), dma((GROUPS, pages, 2)), dma((GROUPS, pages, 2)),
            dma((pages,)), dma((pages,)), dma((7,)), dma((7,)), dma((2,)), dma((2,)),
        ],
        params=dict(collective_id=1, has_side_effects=True, vmem_limit_bytes=64 << 20),
        name="attention_reduce",
    )(q, k, v, ctx, dctx, gm1, xall, *ws, p, *views, gvf, gbin)
    return res[:6], res[6], res[7]


SWAP_X = [(0, 2), (2, 0), (1, 3), (3, 1)]
SWAP_C = [(0, 1), (1, 0), (2, 3), (3, 2)]


def swap(value, pairs):
    return lax.ppermute(value, "seq", pairs)


def per_device(
    fsdp, inputs, lengths, w_query, b_query, w_key, w_value, b_value, w_out, b_out,
    gain_one, shift_one, w_inner, b_inner, w_outer, b_outer, gain_two, shift_two, cotangent,
):
    pages_all, blk, d = inputs.shape
    pages = pages_all // 2
    s = lax.axis_index("seq")
    x_at = lax.div(s, 2)
    direct = fsdp == 8
    ws = (w_query, w_key, w_value, w_out, w_inner, w_outer)
    shards = [w.shape for w in ws]
    width = b_query.shape[0]
    names = (b_query, b_value, b_out, gain_one, shift_one, b_outer, gain_two, shift_two)

    def pages_of(array, side):
        return lax.dynamic_slice_in_dim(array, side * pages, pages, 0)

    order = jnp.stack([s, s ^ 2, s ^ 1, s ^ 3]).astype(jnp.int32)
    thr = pages_of(lengths, x_at).astype(jnp.int32)[:, None] - order[None, :] * blk
    if direct:
        lanes = tuple(v.reshape(1, -1) for v in names + (b_inner,))
        full, rest = fwd(thr, inputs, cotangent, ws, lanes)
        xall, q, k, v, ctx, p, dctx, gm1, dwo, dwi, dw2, output, gv_ffn, gbin = rest
    else:
        wq, wk, wv, wo, wi, w2 = [lax.all_gather(w, "fsdp", axis=0, tiled=True) for w in ws]
        vec = jnp.concatenate(names + (b_inner,)).reshape(12, width)
        gvec = lax.all_gather(vec, "fsdp", axis=0)
        vec_full = jnp.swapaxes(gvec[:, :8], 0, 1).reshape(8, d).astype(F32)
        bin_full = gvec[:, 8:].reshape(1, -1).astype(F32)

        def own_rows(array):
            other = swap(pages_of(array, 1 - x_at), SWAP_X)
            return jnp.concatenate([pages_of(array, x_at), other], axis=1)

        xown, cown = own_rows(inputs), own_rows(cotangent)
        xall = jnp.concatenate([xown, swap(xown, SWAP_C)], axis=1)
        q, k, v, p, ctx = attn_fwd(thr, xall, wq, wk, wv, vec_full)
    if direct:
        tot, grad_inputs, tvec = bwd(
            q, k, v, ctx, dctx, gm1.reshape(pages, 2 * blk, d), xall, full, p, (dwo, dwi, dw2), gv_ffn, gbin, shards
        )
        small = [tvec[i, :width] for i in range(8)]
        g_bi = tvec[8:11].reshape(-1)
    else:
        out, gm1, dctx, dwo, dwi, dw2, gv_ffn, gbin = ffn(ctx, xall, cown, wo, wi, w2, vec_full, bin_full)
        dq, dk, dk_send, dv, dv_send = attn_bwd(q, k, v, p, ctx, dctx)
        dkr, dvr = swap(dk_send, SWAP_C), swap(dv_send, SWAP_C)
        gx_a, gx_b, dwq, dwk, dwv, gv_proj = proj(xall, dq, dk, dkr, dv, dvr, gm1, wq, wk, wv)
        gv = jnp.concatenate([gv_proj[:2], gv_ffn[2:]], axis=0)
        by_owner = jnp.concatenate(
            [jnp.swapaxes(gv.reshape(8, fsdp, width), 0, 1), gbin.reshape(fsdp, 4, width)], axis=1
        )
        tot = [
            lax.psum(lax.psum_scatter(g, "fsdp", scatter_dimension=0, tiled=True), "seq").astype(F32)
            for g in (dwq, dwk, dwv, dwo, dwi, dw2)
        ]
        tvec = lax.psum(lax.psum_scatter(by_owner, "fsdp", scatter_dimension=0, tiled=True)[0], "seq")

        def joined(mine, other):
            here = lax.dynamic_update_slice_in_dim(
                jnp.zeros((pages_all, blk, d), mine.dtype), mine, x_at * pages, 0
            )
            return lax.dynamic_update_slice_in_dim(here, other, (1 - x_at) * pages, 0)

        output = joined(out[:, :blk], swap(out[:, blk:], SWAP_X))
        grad_inputs = joined(gx_a, swap(gx_b, SWAP_X).astype(F32))
        small = [tvec[i] for i in range(8)]
        g_bi = tvec[8:].reshape(-1)
    g_bq, g_bv, g_bo, g_g1, g_s1, g_bo2, g_g2, g_s2 = small
    t_q, t_k, t_v, t_o, t_i, t_2 = tot
    return (
        output, grad_inputs, t_q, g_bq, t_k, t_v, g_bv, t_o, g_bo, g_g1, g_s1,
        t_i, g_bi, t_2, g_bo2, g_g2, g_s2,
    )


def solution(mesh):
    vec, mat, act = P("fsdp"), P("fsdp", None), P("fsdp", "seq", None)
    return jax.shard_map(
        functools.partial(per_device, mesh.shape["fsdp"]),
        mesh=mesh,
        in_specs=(act, vec, mat, vec, mat, mat, vec, mat, vec, vec, vec, mat, vec, mat, vec, vec, vec, act),
        out_specs=(act, act, mat, vec, mat, mat, vec, mat, vec, vec, vec, mat, vec, mat, vec, vec, vec),
        check_vma=False,
    )
```

profile of v0, /device:TPU:0, one launch (start us, length us, event | category | flops | bytes accessed | tf_op | source)
XLA Modules:
  0.0 236.9 jit_solution(6311369068142503473)
XLA Ops:
  0.7 0.1 add_multiply_fusion
  0.7 0.7 dynamic_slice.3
  1.5 0.6 broadcast_subtract_fusion.thr
  2.1 1.2 reshape.128.refs_8_
  3.4 122.2 %gather_forward.1 = (bf16[4,2,96,768]{3,2,1,0:T(8,128)(2,1)}, bf16[4,2,96,768]{3,2,1,0:T(8,128)(2,1)}, bf16[4,2,96,768]{3,2,1,0:T(8,128)(2,1)}, bf16[3,512,768]{...) custom-call(s32[3,4]{1,0:T(4,128)} %broadcast_subtract_fusion.thr, ...), custom_call_target="tpu_custom_call" | custom-call | flops 27179089920 | bytes 14155776 | tf_op jit(solution)/shard_map/gather_forward/pallas_call | solution.py:855
  125.6 99.0 %attention_reduce.1 = (f32[96,768]{1,0:T(8,128)}, f32[96,768]{1,0:T(8,128)}, f32[96,768]{1,0:T(8,128)}, f32[96,768]{1,0:T(8,128)}, f32[96,3072]{1,0:T(8,128)}, /...) custom-call(bf16[3,256,768]{2,1,0:T(8,128)(2,1)} %get-tuple-element.43.q_h, ...), custom_call_target="tpu_custom_call" | custom-call | flops 8455716864 | bytes 84934656 | tf_op jit(solution)/shard_map/attention_reduce/pallas_call | solution.py:1370
  224.6 1.3 slice_bitcast_fusion
  225.8 1.5 slice_bitcast_fusion.1
  227.3 0.0 copy-start
  227.3 2.5 %copy.43 = bf16[6,128,768]{2,1,0:T(8,128)(2,1)} copy(bf16[6,128,768]{2,1,0:T(8,128)(2,1)} %get-tuple-element.92) | data formatting | bytes 2359296
  229.8 0.0 copy-done
  229.8 0.0 copy-start.6
  229.9 0.0 copy-start.5
  229.9 0.0 copy-start.4
  229.9 1.4 copy.44
  231.3 0.0 copy-done.6
  231.3 0.0 copy-start.3
  231.3 0.0 copy-start.2
  231.3 0.7 copy.45
  232.0 0.0 copy-done.5
  232.0 0.7 copy.46
  232.7 0.0 copy-done.4
  232.7 0.7 copy.47
  233.4 0.0 copy-done.3
  233.4 0.7 copy.48
  234.1 0.0 copy-done.2
  234.1 0.0 copy-start.1
  234.1 1.0 copy.49
  235.2 0.7 copy-done.1
  235.8 1.0 copy.50
Async XLA Ops:
  227.3 2.5 %copy-start = (f32[6,128,768]{2,1,0:T(8,128)S(1)}, f32[6,128,768]{2,1,0:T(8,128)}, u32[]{:S(2)}) copy-start(f32[6,128,768]{2,1,0:T(8,128)} %get-tuple-element.93) | copy-start | bytes 7077892
  229.8 1.4 copy-start.6
  229.9 2.1 copy-start.5
  229.9 2.9 %copy-start.4 = (f32[96,768]{1,0:T(8,128)S(1)}, f32[96,768]{1,0:T(8,128)}, u32[]{:S(2)}) copy-start(f32[96,768]{1,0:T(8,128)} %get-tuple-element.97) | copy-start | bytes 884740
  231.3 2.2 copy-start.3
  231.3 2.9 %copy-start.2 = (f32[96,3072]{1,0:T(8,128)S(1)}, f32[96,3072]{1,0:T(8,128)}, u32[]{:S(2)}) copy-start(f32[96,3072]{1,0:T(8,128)} %get-tuple-element.103) | copy-start | bytes 3538948
  234.1 1.7 copy-start.1
where the time goes:
time: 237 us
  Pallas kernels  221 us (93%)
  local copies, waits for them, and re-layouts  14.2 us (6%)
    pallas_call x1, Pallas kernels, fwd(): call(fwd_body, (n * d * (12 * ff + 12 * d), sum((16 * w.size for w in ws)...  122 us
    pallas_call x1, Pallas kernels, bwd(): call(bwd_body, (12 * n * d * d + pages * 10 * own * rows * d, sum((16 * g...  99 us
    unnamed x22, local copies, waits for them, and re-layouts  9.5 us

commit v1 on v0

--- a/solution.py
+++ b/solution.py
@@ -518,7 +518,7 @@
 
 
 def fwd_body(
-    thr, x_in, cot, wq, wk, wv, wo, wi, w2, *refs,
+    lens, x_in, cot, wq, wk, wv, wo, wi, w2, *refs,
 ):
     smalls = refs[:9]
     (
@@ -538,7 +538,7 @@
     for i in range(8):
         vpk[i : i + 1, :width] = smalls[i][...].astype(F32).reshape(1, width)
     for i in range(3):
-        vpk[8 + i : 9 + i, :] = smalls[8][:, 128 * i : 128 * (i + 1)].astype(F32).reshape(1, 128)
+        vpk[8 + i : 9 + i, :] = smalls[8][128 * i : 128 * (i + 1)].astype(F32).reshape(1, 128)
     gvec[f] = vpk[...]
     x_peer, c_peer = at(z, y, 1 - x, c), at(z, y, x, 1 - c)
     meet([{"fsdp": lax.rem(f + k + 1, 8)} for k in range(7)] + [x_peer, c_peer])
@@ -591,7 +591,10 @@
     place_row = lax.broadcasted_iota(jnp.int32, (blk, own), 0)
     for page in range(pages):
         for b in range(4):
-            bias[page, b * blk : (b + 1) * blk, :] = jnp.where(place_row < thr[page, b], 0.0, NEG)
+            side = x if b % 2 == 0 else 1 - x
+            core = c if b < 2 else 1 - c
+            limit = lens[pages * x + page] - (2 * side + core) * blk
+            bias[page, b * blk : (b + 1) * blk, :] = jnp.where(place_row < limit, 0.0, NEG)
     each(0, "forward")
     each(1, "along_z")
     each(0, "along_y")
@@ -621,7 +624,7 @@
     each(0, "arrive")
 
     low_lane = lax.broadcasted_iota(jnp.int32, (own, PAIR), 1) < HEAD_DIM
-    stages = (("along_z", 1 - 8 * EARLY // 3), ("forward", 0), ("along_y", 2), ("along_x", 5), ("to_core", 8))
+    stages = (("along_z", 1 - 8 * EARLY // 3), ("forward", 0), ("along_y", 3), ("along_x", 8), ("to_core", 13))
 
     def tick(t):
         for step, late in stages:
@@ -843,7 +846,7 @@
     back_out.wait()
 
 
-def fwd(thr, x_in, cot, ws, smalls):
+def fwd(lens, x_in, cot, ws, smalls):
     pages_all, blk, d = x_in.shape
     pages, own, rows = pages_all // 2, 2 * blk, 4 * blk
     n = pages * own
@@ -880,7 +883,7 @@
         + [dma((5,)), dma((5,)), dma((3,)), dma((7,)), dma((7,)), dma((2,)), dma((11,)), dma((2, 2))],
         params=dict(collective_id=0, has_side_effects=True, vmem_limit_bytes=64 << 20),
         name="gather_forward",
-    )(thr, x_in, cot, *ws, *smalls)
+    )(lens, x_in, cot, *ws, *smalls)
     full = [r.reshape(d, d) for r in res[:3]]
     return full, res[3:]
 
@@ -1142,8 +1145,8 @@
             else:
                 getattr(gfold(g, w), name)()
 
-    stages = (("over_x", 0), ("over_y", 6), ("over_z", 14), ("inside", 19), ("total", 23), ("write", 28))
-    pace = 3
+    stages = (("over_x", 0), ("over_y", 3), ("over_z", 7), ("inside", 10), ("total", 13), ("write", 16))
+    pace = 2
     last = pace * (REST + GROUPS - 1) + stages[-1][1] + 1
 
     def tick(t):
@@ -1398,6 +1401,41 @@
     return res[:6], res[6], res[7]
 
 
+def finish_body(*refs):
+    n = 8
+    src, small, dst, lows = refs[:n], refs[n], refs[n + 1 : 2 * n + 1], refs[2 * n + 1 : 2 * n + 10]
+    held, sem_in, sem_out = refs[2 * n + 10 : 3 * n + 10], refs[-2], refs[-1]
+    loads = [pltpu.make_async_copy(src[i], held[i], sem_in.at[i]) for i in range(n)]
+    stores = [pltpu.make_async_copy(held[i], dst[i], sem_out.at[i]) for i in range(n)]
+    for copy in loads:
+        copy.start()
+    width = lows[0].shape[0]
+    for i in range(8):
+        lows[i][...] = small[i, :width]
+    for i in range(3):
+        lows[8][128 * i : 128 * (i + 1)] = small[8 + i, :]
+    for load, store in zip(loads, stores):
+        load.wait()
+        store.start()
+    for copy in stores:
+        copy.wait()
+
+
+def finish(arrays, small, width, wide):
+    sds = jax.ShapeDtypeStruct
+    dma = pltpu.SemaphoreType.DMA
+    n = len(arrays)
+    return call(
+        finish_body,
+        (0, 2 * sum(a.size * a.dtype.itemsize for a in arrays), 0),
+        in_specs=[ANY] * n + [VM],
+        out_specs=[ANY] * n + [VM] * 9,
+        out_shape=[sds(a.shape, a.dtype) for a in arrays] + [sds((width,), F32)] * 8 + [sds((wide,), F32)],
+        scratch_shapes=[pltpu.VMEM(a.shape, a.dtype) for a in arrays] + [dma((n,)), dma((n,))],
+        name="finish",
+    )(*arrays, small)
+
+
 SWAP_X = [(0, 2), (2, 0), (1, 3), (3, 1)]
 SWAP_C = [(0, 1), (1, 0), (2, 3), (3, 2)]
 
@@ -1426,8 +1464,7 @@
     order = jnp.stack([s, s ^ 2, s ^ 1, s ^ 3]).astype(jnp.int32)
     thr = pages_of(lengths, x_at).astype(jnp.int32)[:, None] - order[None, :] * blk
     if direct:
-        lanes = tuple(v.reshape(1, -1) for v in names + (b_inner,))
-        full, rest = fwd(thr, inputs, cotangent, ws, lanes)
+        full, rest = fwd(lengths.astype(jnp.int32), inputs, cotangent, ws, names + (b_inner,))
         xall, q, k, v, ctx, p, dctx, gm1, dwo, dwi, dw2, output, gv_ffn, gbin = rest
     else:
         wq, wk, wv, wo, wi, w2 = [lax.all_gather(w, "fsdp", axis=0, tiled=True) for w in ws]
@@ -1447,8 +1484,8 @@
         tot, grad_inputs, tvec = bwd(
             q, k, v, ctx, dctx, gm1.reshape(pages, 2 * blk, d), xall, full, p, (dwo, dwi, dw2), gv_ffn, gbin, shards
         )
-        small = [tvec[i, :width] for i in range(8)]
-        g_bi = tvec[8:11].reshape(-1)
+        res = finish((output, grad_inputs) + tuple(tot), tvec, width, b_inner.shape[0])
+        output, grad_inputs, tot, small, g_bi = res[0], res[1], res[2:8], res[8:16], res[16]
     else:
         out, gm1, dctx, dwo, dwi, dw2, gv_ffn, gbin = ffn(ctx, xall, cown, wo, wi, w2, vec_full, bin_full)
         dq, dk, dk_send, dv, dv_send = attn_bwd(q, k, v, p, ctx, dctx)

time: 237 us -> 217 us (0.916)
  local copies, waits for them, and re-layouts: 14.2 us -> 0 us
  Pallas kernels: 221 us -> 216 us
    unnamed x22 -> x0, local copies, waits for them, and re-layouts: 9.5 us -> none
    pallas_call x1, Pallas kernels: 122 us -> 114 us  [fwd(): call(fwd_body, (n * d * (12 * ff + 12 * d), sum((16 * w.size for w in ws)...]
    pallas_call x0 -> x1, Pallas kernels: none -> 7.11 us  [finish(): call(finish_body, (0, 2 * sum((a.size * a.dtype.itemsize for a in arrays)...]
    pallas_call x1, Pallas kernels: 99 us -> 94.5 us  [bwd(): call(bwd_body, (12 * n * d * d + pages * 10 * own * rows * d, sum((16 * g...]
    reshape x2 -> x0, local copies, waits for them, and re-layouts: 2.5 us -> none  [the longest x1 1.26 us: per_device(): g_bi = tvec[8:11].reshape(-1)]
where the time goes in v1:
time: 217 us
  Pallas kernels  216 us (100%)
    pallas_call x1, Pallas kernels, fwd(): call(fwd_body, (n * d * (12 * ff + 12 * d), sum((16 * w.size for w in ws)...  114 us
    pallas_call x1, Pallas kernels, bwd(): call(bwd_body, (12 * n * d * d + pages * 10 * own * rows * d, sum((16 * g...  94.5 us
    pallas_call x1, Pallas kernels, finish(): call(finish_body, (0, 2 * sum((a.size * a.dtype.itemsize for a in arrays)...  7.11 us

profile of v1, /device:TPU:0, one launch (start us, length us, event | category | flops | bytes accessed | tf_op | source)
XLA Modules:
  0.0 216.6 jit_solution(7039269242610775879)
XLA Ops:
  0.7 114.1 %gather_forward.1 = (bf16[4,2,96,768]{3,2,1,0:T(8,128)(2,1)}, bf16[4,2,96,768]{3,2,1,0:T(8,128)(2,1)}, bf16[4,2,96,768]{3,2,1,0:T(8,128)(2,1)}, bf16[3,512,768]{...) custom-call(s32[6]{0:T(128)} %lens.1, ...), custom_call_target="tpu_custom_call" | custom-call | flops 27179089920 | bytes 14155776 | tf_op jit(solution)/shard_map/gather_forward/pallas_call | solution.py:858
  114.8 94.5 %attention_reduce.1 = (f32[96,768]{1,0:T(8,128)}, f32[96,768]{1,0:T(8,128)}, f32[96,768]{1,0:T(8,128)}, f32[96,768]{1,0:T(8,128)}, f32[96,3072]{1,0:T(8,128)}, /...) custom-call(bf16[3,256,768]{2,1,0:T(8,128)(2,1)} %get-tuple-element.60.q_h, ...), custom_call_target="tpu_custom_call" | custom-call | flops 8455716864 | bytes 84934656 | tf_op jit(solution)/shard_map/attention_reduce/pallas_call | solution.py:1373
  209.3 7.1 %finish.1 = (bf16[6,128,768]{2,1,0:T(8,128)(2,1)}, f32[6,128,768]{2,1,0:T(8,128)}, f32[96,768]{1,0:T(8,128)}, f32[96,768]{1,0:T(8,128)}, f32[96,768]{1,0:T(8,128...) custom-call(bf16[6,128,768]{2,1,0:T(8,128)(2,1)} %get-tuple-element., ...), custom_call_target="tpu_custom_call" | custom-call | bytes 14155776 | tf_op jit(solution)/shard_map/finish/pallas_call | solution.py:1428

commit v2 on v1

--- a/solution.py
+++ b/solution.py
@@ -522,14 +522,15 @@
 ):
     smalls = refs[:9]
     (
-        gq_h, gk_h, gv_h, xall_h, q_h, k_h, v_h, c_h, p_o, dctx_h, gm1_h, dwo_h, dwi_h, dw2_h, fin_out, gvs, gbin,
-    ) = refs[9:26]
+        gq_h, gk_h, gv_h, xall_h, q_h, k_h, v_h, c_h, p_o,
+        go_h, gi_h, g2_h, act_h, dd_h, hid_h, gout_h, n1_h, gm2_h, r1_h, out_h, gvs, vec,
+    ) = refs[9:31]
     (
-        gq, gk, gv, go, gi, g2, xall, q_o, k_o, v_o, c_o, cown, bias, pbuf, vpk, gvec, vec, b_in,
-        act, dd, hid, gout, gatt, dctx, n1s, accs, r1s, dw2_s, dwi_s,
-    ) = refs[26:55]
-    qs, rs = refs[55:65], refs[65:75]
-    asend, arecv, aloc, vs, vr, ps, outs_sem, grad_sem = refs[75:]
+        gq, gk, gv, go, gi, g2, xall, q_o, k_o, v_o, c_o, cown, bias, pbuf, vpk, gvec, b_in,
+        act, dd, hid, gout, n1b, n1s, accs, r1s,
+    ) = refs[31:56]
+    qs, rs = refs[56:66], refs[66:76]
+    asend, arecv, aloc, vs, vr, ps, outs_sem, chunk_sem = refs[76:]
     z, y, x, c = where = place()
     f = 2 * z + y
     pages, rows = xall.shape[0], xall.shape[1]
@@ -724,16 +725,26 @@
         return ref[...].reshape(d, d)
 
     rest(0, "arrive")
+    later = [pltpu.make_async_copy(go, go_h, outs_sem.at[8])]
+    later[0].start()
     for page in range(pages):
         r = slice(page * own, (page + 1) * own)
         mid = xall[page, :own].astype(F32) + (dot(c_o[page], square(go)) + vec[2:3, :])
         n1, r1 = row_norm(mid)
         n1s[r, :] = n1
+        n1b[r, :] = n1.astype(BF)
         r1s[r, :] = jnp.broadcast_to(r1, (own, 128))
         hid[r, :] = (n1 * vec[3:4, :] + vec[4:5, :]).astype(BF)
 
     def ticks(lo, hi):
         lax.fori_loop(lo, hi, lambda t, carry: (tick(t), carry)[1], 0)
+
+    def chunk_stores(j):
+        cols = pl.ds(pl.multiple_of(j * d, d), d)
+        return [
+            pltpu.make_async_copy(src, dst.at[j], chunk_sem.at[i, j])
+            for i, (src, dst) in enumerate(((gi.at[j], gi_h), (act.at[:, cols], act_h), (dd.at[:, cols], dd_h)))
+        ]
 
     def up(j, carry):
         ticks(n_ticks + 3 * j, jnp.minimum(n_ticks + 3 * j + 3, last))
@@ -743,6 +754,8 @@
         big, bell = normal_parts(pre)
         act[:, cols] = (pre * big).astype(BF)
         dd[:, cols] = (big + pre * bell).astype(BF)
+        for copy in chunk_stores(j):
+            copy.start()
         return carry
 
     lax.fori_loop(0, n_chunks, up, 0)
@@ -752,6 +765,8 @@
     keep_c.wait()
     cot_b.wait_recv()
     stores[0].wait()
+    later.append(pltpu.make_async_copy(g2, g2_h, outs_sem.at[9]))
+    later[1].start()
 
     def w2_rows(j):
         return g2[j].reshape(d, d)
@@ -778,59 +793,9 @@
         add(5, gob.astype(F32))
         add(6, ct * n2)
         add(7, ct)
-    keep_out = pltpu.make_async_copy(q_o.at[:, pl.ds(0, blk), :], fin_out.at[mine], aloc.at[2])
-    back_out = remote(q_o.at[:, pl.ds(blk, blk), :], fin_out.at[mine], asend.at[4], arecv.at[4], x_peer)
-    keep_out.start()
-    back_out.start()
-
-    def grad_store(j, i):
-        slot = lax.rem(j, 2)
-        return pltpu.make_async_copy((dw2_s, dwi_s)[i].at[slot], (dw2_h, dwi_h)[i].at[j], grad_sem.at[i, slot])
-
-    def down(j, carry):
-        cols = pl.ds(pl.multiple_of(j * d, d), d)
-        di = (dot(gout[...], w2_rows(j), NT) * dd[:, cols].astype(F32)).astype(BF)
-        dd[:, cols] = di
-        accs[...] += dot(di, gi[j].reshape(d, d), NT)
-        gbin[:, cols] = jnp.sum(di.astype(F32), 0, keepdims=True)
-
-        @pl.when(j >= 2)
-        def _():
-            grad_store(j, 0).wait()
-            grad_store(j, 1).wait()
-
-        slot = lax.rem(j, 2)
-        dw2_s[slot] = dot(act[:, cols], gout[...], TN).astype(BF)
-        dwi_s[slot] = dot(hid[...], di, TN).astype(BF)
-        grad_store(j, 0).start()
-        grad_store(j, 1).start()
-        return carry
-
-    lax.fori_loop(0, n_chunks, down, 0)
-    for page in range(pages):
-        r = slice(page * own, (page + 1) * own)
-        gh = accs[r, :]
-        n1 = n1s[r, :]
-        gm1 = norm_back(gh * vec[3:4, :], n1, r1s[r, 0:1])
-        accs[r, :] = gm1
-        ga = gm1.astype(BF)
-        gatt[r, :] = ga
-        dctx[page] = dot(ga, square(go), NT).astype(BF)
-        add(2, ga.astype(F32))
-        add(3, gh * n1)
-        add(4, gh)
-    tail = [
-        pltpu.make_async_copy(accs, gm1_h, outs_sem.at[8]),
-        pltpu.make_async_copy(dctx, dctx_h, outs_sem.at[9]),
-        pltpu.make_async_copy(hid, dwo_h, outs_sem.at[10]),
-    ]
-    tail[0].start()
-    tail[1].start()
-    hid[...] = dot(c_o[...].reshape(pages * own, d), gatt[...], TN).astype(BF)
-    tail[2].start()
-    for j in range(n_chunks - 2, n_chunks):
-        grad_store(j, 0).wait()
-        grad_store(j, 1).wait()
+    for i, (src, dst) in enumerate(((accs, gm2_h), (gout, gout_h), (hid, hid_h), (n1b, n1_h), (r1s, r1_h), (q_o, out_h))):
+        later.append(pltpu.make_async_copy(src, dst, outs_sem.at[10 + i]))
+        later[-1].start()
 
     def finish(p, carry):
         rest(p, "drain")
@@ -841,9 +806,10 @@
         each(g, "drain")
     for copy in vecs + [to_b, to_c, to_d, cot_b]:
         copy.wait_send()
-    for copy in stores[1:] + tail + [keep_out]:
+    for j in range(n_chunks):
+        later += chunk_stores(j)
+    for copy in stores[1:] + later:
         copy.wait()
-    back_out.wait()
 
 
 def fwd(lens, x_in, cot, ws, smalls):
@@ -859,33 +825,33 @@
         fwd_body,
         (n * d * (12 * ff + 12 * d), sum(16 * w.size for w in ws), pages * HEADS * own * rows),
         in_specs=[pl.BlockSpec(memory_space=pltpu.SMEM)] + [ANY] * 5 + [VM] * 12,
-        out_specs=[ANY] * 15 + [VM, VM],
+        out_specs=[ANY] * 20 + [VM, VM],
         out_shape=[sds(quarter, BF)] * 3
         + [
             sds((pages, rows, d), BF),
             sds((pages, own, d), BF), sds((pages, rows, d), BF), sds((pages, rows, d), BF), sds((pages, own, d), BF),
             sds((pages, HEADS, rows, own), BF),
-            sds((pages, own, d), BF), sds((n, d), F32), sds((d, d), BF),
-            sds((ff // d, d, d), BF), sds((ff // d, d, d), BF), sds((pages_all, blk, d), BF),
-            sds((8, d), F32), sds((1, ff), F32),
+            sds(quarter, BF), sds((ff // d,) + quarter, BF), sds((4, 2, ff // 8, d), BF),
+            sds((ff // d, n, d), BF), sds((ff // d, n, d), BF), sds((n, d), BF), sds((n, d), BF), sds((n, d), BF),
+            sds((n, d), F32), sds((n, 128), F32), sds((pages, own, d), BF),
+            sds((8, d), F32), sds((8, d), F32),
         ],
         scratch_shapes=[
             vm(quarter, BF), vm(quarter, BF), vm(quarter, BF), vm(quarter, BF),
             vm((ff // d,) + quarter, BF), vm((4, 2, ff // 8, d), BF),
             vm((pages, rows, d), BF), vm((pages, own, d), BF), vm((pages, rows, d), BF), vm((pages, rows, d), BF),
             vm((pages, own, d), BF), vm((pages, own, d), BF), vm((pages, rows, own), F32), vm((2, 2, rows, own), BF),
-            vm((16, 128), F32), vm((8, 16, 128), F32), vm((8, d), F32), vm((1, ff), F32),
-            vm((n, ff), BF), vm((n, ff), BF), vm((n, d), BF), vm((n, d), BF), vm((n, d), BF), vm((pages, own, d), BF),
-            vm((n, d), F32), vm((n, d), F32), vm((n, 128), F32), vm((2, d, d), BF), vm((2, d, d), BF),
+            vm((16, 128), F32), vm((8, 16, 128), F32), vm((1, ff), F32),
+            vm((n, ff), BF), vm((n, ff), BF), vm((n, d), BF), vm((n, d), BF), vm((n, d), BF),
+            vm((n, d), F32), vm((n, d), F32), vm((n, 128), F32),
         ]
         + spread_sems(GROUPS, 3)
         + spread_sems(REST)
-        + [dma((5,)), dma((5,)), dma((3,)), dma((7,)), dma((7,)), dma((2,)), dma((11,)), dma((2, 2))],
+        + [dma((5,)), dma((5,)), dma((3,)), dma((7,)), dma((7,)), dma((2,)), dma((16,)), dma((3, ff // d))],
         params=dict(collective_id=0, has_side_effects=True, vmem_limit_bytes=64 << 20),
         name="gather_forward",
     )(lens, x_in, cot, *ws, *smalls)
-    full = [r.reshape(d, d) for r in res[:3]]
-    return full, res[3:]
+    return res
 
 
 class Fold:
@@ -1003,9 +969,8 @@
         view[...] = self.fin[...].astype(F32) + self.rf[...].astype(F32)
         self.ecopy(view).start()
 
-    def drain(self, first, view):
+    def drain(self, view):
         self.ecopy(view).wait_recv()
-        first.wait_send()
         self.xcopy().wait_send()
         self.ycopy().wait_send()
         self.a().wait_send()
@@ -1043,58 +1008,48 @@
 
 
 def bwd_body(
-    q_h, k_h, v_h, c_h, dc_h, g1_h, x_h, gq_h, gk_h, gv_h, p_h, dwo, dwi, dw2, gvf, gbin,
-    oq, ok, ov, oo, oi, o2, gx, ovec,
+    gq_h, gk_h, gv_h, x_h, q_h, k_h, v_h, c_h, p_h, go_h, gi_h, g2_h, act_h, dd_h, hid_h, gout_h, n1_h, gm2_h, r1_h, out_h,
+    gvf, vec,
+    oq, ok, ov, oo, oi, o2, gx, fin_out, ovec,
     *refs,
 ):
-    q_v, k_v, v_v, c_v, dc_v, g1_v, x_v, gq_v, gk_v, gv_v = refs[:10]
-    (acc, dwg, dq_all, dk_all, dv_all, rk, rv, sk, sv, pbuf, x_t, gxs, rgx, pack, vecin, vtot, vx, brow) = refs[10:28]
-    fb, gb = refs[28:34], refs[34:40]
-    fsem, gsem = refs[40:52], refs[52:64]
-    lsem, csem, ps, ks, kr, gs, gr, vs, vr, us, ur = refs[64:]
+    (
+        pool, hid, gout, go, n1b, accs, r1s, c_v, dc_v, acc, dwg, st, dq_all, dk_all, dv_all, rk, rv, sk, sv, pbuf,
+        rgx, pack, vecin, vtot, vx, brow, gvs, gbin, stay,
+    ) = refs[:29]
+    fb, gb = refs[29:35], refs[35:41]
+    fsem, gsem = refs[41:53], refs[53:65]
+    lsem, msem, ssem, ps, ks, kr, gs, gr, os, vs, vr, us, ur, bs, br, bl = refs[65:]
     z, y, x, c = where = place()
     f = 2 * z + y
-    pages, own, d = q_h.shape
+    pages, own, d = c_h.shape
+    n = pages * own
     blk = own // 2
-    rows = k_h.shape[1]
+    rows = 2 * own
+    at_k, at_v, at_q, at_gq, at_gk, at_gv = 0, 2 * n, 4 * n, 5 * n, 6 * n, 7 * n
     x_peer, c_peer = at(z, y, 1 - x, c), at(z, y, x, 1 - c)
     meet([{"fsdp": lax.rem(f + k + 1, 8)} for k in range(7)] + [x_peer, c_peer])
 
-    def first_of(p):
-        def run(src, row0, col0, go):
-            rr = pl.ds(row0, ROW)
-            mine = src.at[:, :, rr, pl.ds(pl.multiple_of(col0 + 384 * c, 128), 384)]
-            other = src.at[:, :, rr, pl.ds(pl.multiple_of(col0 + 384 * (1 - c), 128), 384)]
-            copy = pltpu.make_async_copy(mine, acc.at[p], csem.at[p])
-            send = remote(other, fb[0].at[p], fsem[0].at[p], fsem[1].at[p], c_peer)
-            if go:
-                copy.start()
-                send.start()
-            return copy, send
-
-        return run
-
-    def rest_src(p, run):
-        @pl.when(p < 4)
-        def _():
-            run(dw2, ROW * p, 0)
-
-        @pl.when(jnp.logical_and(p >= 4, p < 8))
-        def _():
-            run(dwi.at[p - 4], 0, 0)
-
-        @pl.when(p == 8)
-        def _():
-            run(dwo, 0, 0)
+    def other_half(p, run):
+        @pl.when(p < 6)
+        def _():
+            run(dwg.at[lax.div(p, 2), :, :, :, pl.ds(pl.multiple_of(384 * lax.rem(p, 2), 128), 384)])
+
+        @pl.when(p >= 6)
+        def _():
+            run(st.at[p - 6])
+
+    def launch(p):
+        other_half(p, lambda ref: remote(ref, fb[0].at[p], fsem[0].at[p], fsem[1].at[p], c_peer).start())
 
     def rest_out(p, run):
         @pl.when(p < 4)
         def _():
-            run(o2.at[pl.ds(pl.multiple_of(ROW * p, 32), ROW), pl.ds(pl.multiple_of(384 * c, 128), 384)])
+            run(oi.at[:, pl.ds(pl.multiple_of(768 * p + 384 * c, 128), 384)])
 
         @pl.when(jnp.logical_and(p >= 4, p < 8))
         def _():
-            run(oi.at[:, pl.ds(pl.multiple_of(768 * (p - 4) + 384 * c, 128), 384)])
+            run(o2.at[pl.ds(pl.multiple_of(ROW * (p - 4), 32), ROW), pl.ds(pl.multiple_of(384 * c, 128), 384)])
 
         @pl.when(p == 8)
         def _():
@@ -1111,25 +1066,22 @@
 
         @pl.when(ok_p)
         def _():
-            if name == "start":
-                rest_src(p, lambda src, r0, c0: first_of(p)(src, r0, c0, True) and None)
-            elif name == "over_x":
-                pltpu.make_async_copy(acc.at[p], acc.at[p], csem.at[p]).wait()
+            if name == "over_x":
                 fold(p).over_x(any_first(p))
             elif name == "write":
                 rest_out(p, lambda view: fold(p).write(view))
             elif name == "drain":
-                rest_out(p, lambda view: fold(p).drain(any_first(p), view))
+                rest_out(p, lambda view: fold(p).drain(view))
             else:
                 getattr(fold(p), name)()
 
     def gfold(g, w):
-        cols = pl.ds(pl.multiple_of(128 * c, 128), 128)
-        return Fold(where, lambda sel: dwg.at[(g, w) + sel + (cols,)], gb, gsem, (g, w), KEEP_GROUP)
+        cols = pl.ds(pl.multiple_of(GCOLS * w + 128 * c, 128), 128)
+        return Fold(where, lambda sel: dwg.at[(g,) + sel + (cols,)], gb, gsem, (g, w), KEEP_GROUP)
 
     def gfirst(g, w):
-        cols = pl.ds(pl.multiple_of(128 * (1 - c), 128), 128)
-        return remote(dwg.at[g, w, :, :, :, cols], gb[0].at[g, w], gsem[0].at[g, w], gsem[1].at[g, w], c_peer)
+        cols = pl.ds(pl.multiple_of(GCOLS * w + 128 * (1 - c), 128), 128)
+        return remote(dwg.at[g, :, :, :, cols], gb[0].at[g, w], gsem[0].at[g, w], gsem[1].at[g, w], c_peer)
 
     def gstep(g, name):
         for w, o in enumerate((oq, ok, ov)):
@@ -1141,12 +1093,13 @@
             elif name == "write":
                 gfold(g, w).write(view)
             elif name == "drain":
-                gfold(g, w).drain(gfirst(g, w), view)
+                gfold(g, w).drain(view)
+                gfirst(g, w).wait_send()
             else:
                 getattr(gfold(g, w), name)()
 
-    stages = (("over_x", 0), ("over_y", 3), ("over_z", 7), ("inside", 10), ("total", 13), ("write", 16))
-    pace = 2
+    stages = (("over_x", 0), ("over_y", 4), ("over_z", 10), ("inside", 15), ("total", 19), ("write", 24))
+    pace = 3
     last = pace * (REST + GROUPS - 1) + stages[-1][1] + 1
 
     def tick(t):
@@ -1162,29 +1115,130 @@
                 def _():
                     gstep(p - REST, name)
 
-    loads = [
+    firsts = [
         pltpu.make_async_copy(src, dst, lsem.at[i])
         for i, (src, dst) in enumerate(
-            (
-                (q_h, q_v), (k_h, k_v), (v_h, v_v), (c_h, c_v), (dc_h, dc_v), (x_h.at[:, pl.ds(0, own), :], x_v),
-                (g1_h, g1_v), (gq_h, gq_v), (gk_h, gk_v), (gv_h, gv_v),
-            )
+            ((gout_h, gout), (hid_h, hid), (gm2_h, accs), (n1_h, n1b), (r1_h, r1s), (go_h, go), (c_h, c_v))
         )
+    ]
+
+    def row_block(start, size):
+        return pl.ds(pl.multiple_of(start, 256), size)
+
+    def slot(kind, j):
+        return pool.at[row_block((2 * kind + lax.rem(j, 2)) * n, n), :]
+
+    def chunk_loads(j):
+        return [
+            pltpu.make_async_copy(src.at[j], slot(kind, j), msem.at[kind, lax.rem(j, 2)])
+            for kind, src in enumerate((gi_h, g2_h, act_h, dd_h))
+        ]
+
+    seconds = [
+        pltpu.make_async_copy(src, pool.at[pl.ds(start, src.shape[0]), :], ssem.at[i])
+        for i, (src, start) in enumerate(
+            ((q_h, at_q), (k_h, at_k), (v_h, at_v), (gq_h, at_gq), (gk_h, at_gk), (gv_h, at_gv))
+        )
+    ] + [
+        pltpu.make_async_copy(x_h.at[page, pl.ds(0, own), :], hid.at[pl.ds(page * own, own), :], ssem.at[6 + page])
+        for page in range(pages)
     ]
 
     def p_copy(it, half):
         g, page = lax.div(it, pages), lax.rem(it, pages)
         return pltpu.make_async_copy(p_h.at[page, pl.ds(4 * g + 2 * half, 2)], pbuf.at[half], ps.at[half])
 
+    pages_mine = pl.ds(pages * x, pages)
+    back_out = remote(out_h.at[:, pl.ds(blk, blk), :], fin_out.at[pages_mine], bs.at[0], br.at[0], x_peer)
+    stay_in = pltpu.make_async_copy(out_h.at[:, pl.ds(0, blk), :], stay, bl.at[0])
+    stay_out = pltpu.make_async_copy(stay, fin_out.at[pages_mine], bl.at[1])
+    back_out.start()
+    for copy in firsts[:1]:
+        copy.start()
+    for copy in chunk_loads(0):
+        copy.start()
+    for copy in firsts[1:]:
+        copy.start()
+    for copy in chunk_loads(1):
+        copy.start()
     for half in range(2):
         p_copy(0, half).start()
-    for copy in loads[:5]:
+    stay_in.start()
+    gvs[...] = gvf[...]
+
+    def halves(value):
+        low, high = value[..., :384], value[..., 384:]
+        return jnp.where(c == 0, low, high), jnp.where(c == 0, high, low)
+
+    n_chunks = gi_h.shape[0]
+    firsts[0].wait()
+    firsts[1].wait()
+    firsts[2].wait()
+
+    def down(j, carry):
+        for copy in chunk_loads(j):
+            copy.wait()
+        cols = pl.ds(pl.multiple_of(j * d, d), d)
+        di = (dot(gout[...], slot(1, j)[...], NT) * slot(3, j)[...].astype(F32)).astype(BF)
+        accs[...] += dot(di, slot(0, j)[...], NT)
+        gbin[:, cols] = jnp.sum(di.astype(F32), 0, keepdims=True)
+        keep, pass_on = halves(dot(hid[...], di, TN).astype(BF))
+        acc[j] = keep.reshape(4, 2, ROW, 384)
+        other_half(j, lambda ref: ref.__setitem__(Ellipsis, pass_on.reshape(4, 2, ROW, 384)))
+        launch(j)
+        keep, pass_on = halves(dot(slot(2, j)[...], gout[...], TN).astype(BF))
+        keep, pass_on = keep.reshape(2, 4, ROW, 384), pass_on.reshape(2, 4, ROW, 384)
+        for p in range(4):
+            acc[4 + p, j] = keep[:, p]
+            if p < 2:
+                dwg[2, j, :, :, 384 * p : 384 * p + 384] = pass_on[:, p]
+            else:
+                st[p - 2, j] = pass_on[:, p]
+
+        @pl.when(j + 2 < n_chunks)
+        def _():
+            for copy in chunk_loads(j + 2):
+                copy.start()
+
+        @pl.when(j > 0)
+        def _():
+            lax.fori_loop(pace * (j - 1), pace * j, lambda t, carry: (tick(t), carry)[1], 0)
+
+        return carry
+
+    lax.fori_loop(0, n_chunks, down, 0)
+    for p in range(4):
+        launch(4 + p)
+    stay_in.wait()
+    stay_out.start()
+    for copy in seconds:
         copy.start()
-    for p in range(REST):
-        step(p, "start")
-    for copy in loads[5:]:
-        copy.start()
-    for copy in loads[:5]:
+    for copy in firsts[3:]:
+        copy.wait()
+
+    def add(row, value):
+        gvs[row : row + 1, :] += jnp.sum(value, 0, keepdims=True)
+
+    before = pace * (n_chunks - 1)
+    for page in range(pages):
+        r = slice(page * own, (page + 1) * own)
+        gh = accs[r, :]
+        n1 = n1b[r, :].astype(F32)
+        gm1 = norm_back(gh * vec[3:4, :], n1, r1s[r, 0:1])
+        accs[r, :] = gm1
+        ga = gm1.astype(BF)
+        gout[r, :] = ga
+        dc_v[page] = dot(ga, go[...], NT).astype(BF)
+        add(2, ga.astype(F32))
+        add(3, gh * n1)
+        add(4, gh)
+        tick(before + page)
+    before += pages
+    keep, pass_on = halves(dot(c_v[...].reshape(n, d), gout[...], TN).astype(BF))
+    acc[8] = keep.reshape(4, 2, ROW, 384)
+    st[2] = pass_on.reshape(4, 2, ROW, 384)
+    launch(8)
+    for copy in seconds:
         copy.wait()
 
     low_lane = lax.broadcasted_iota(jnp.int32, (own, PAIR), 1) < HEAD_DIM
@@ -1194,7 +1248,7 @@
         g, page = lax.div(it, pages), lax.rem(it, pages)
         gcols = pl.ds(pl.multiple_of(g * GCOLS, GCOLS), GCOLS)
         return [
-            remote(s_ref.at[page, :, gcols], r_ref.at[page, :, gcols], ks.at[g, page, i], kr.at[g, page, i], c_peer)
+            remote(s_ref.at[page], r_ref.at[page, :, gcols], ks.at[g, page, i], kr.at[g, page, i], c_peer)
             for i, (s_ref, r_ref) in enumerate(((sk, rk), (sv, rv)))
         ]
 
@@ -1202,11 +1256,12 @@
         g, page = lax.div(it, pages), lax.rem(it, pages)
         here = pl.ds(pl.multiple_of(page * own, own), own)
         p_copy(it, half).wait()
+        local = slice(half * PAIR, (half + 1) * PAIR)
         cols = pl.ds(pl.multiple_of(g * GCOLS + half * PAIR, PAIR), PAIR)
-        qp = q_v[page, :, cols] * jnp.array(scale, BF)
-        kp = k_v[page, :, cols]
+        qp = pool[row_block(at_q + page * own, own), cols] * jnp.array(scale, BF)
+        kp = pool[row_block(at_k + page * rows, rows), cols]
         kt = kp.T
-        vp = v_v[page, :, cols]
+        vp = pool[row_block(at_v + page * rows, rows), cols]
         dc = dc_v[page, :, cols]
         prod = (dc.astype(F32) * c_v[page, :, cols].astype(F32)).T
         dk = None
@@ -1228,15 +1283,17 @@
             dqs.append(dot(kt[feats], dst))
         dq_all[here, cols] = (jnp.concatenate(dqs, axis=0) * scale).T.astype(BF)
         dk_all[here, cols] = dk[:own].astype(BF)
-        sk[page, :, cols] = dk[own:].astype(BF)
+        sk[page, :, local] = dk[own:].astype(BF)
         dv_all[here, cols] = dv[:own].astype(BF)
-        sv[page, :, cols] = dv[own:].astype(BF)
+        sv[page, :, local] = dv[own:].astype(BF)
 
         @pl.when(it + 1 < GROUPS * pages)
         def _():
             p_copy(it + 1, half).start()
 
     def group_grads(g):
+        for i in range(2):
+            any_first(2 * g + i).wait_send()
         gcols = pl.ds(pl.multiple_of(g * GCOLS, GCOLS), GCOLS)
         for page in range(pages):
             here = pl.ds(page * own, own)
@@ -1246,27 +1303,41 @@
             dv_all[here, gcols] = dv_all[here, gcols] + rv[page, :, gcols]
         for w, grad in enumerate((dq_all, dk_all, dv_all)):
             value = grad[:, gcols]
-            dwg[g, w] = dot(x_t[...], value).astype(BF).reshape(4, 2, ROW, GCOLS)
+            dwg[g, :, :, :, w * GCOLS : (w + 1) * GCOLS] = (
+                dot(hid[...], value, TN).astype(BF).reshape(4, 2, ROW, GCOLS)
+            )
             if w != 1:
                 brow[w : w + 1, gcols] = jnp.sum(value.astype(F32), 0, keepdims=True)
         gstep(g, "start")
 
     def gx_send(page):
-        return remote(gxs.at[page], rgx.at[page], gs.at[page], gr.at[page], x_peer)
+        return remote(go.at[pl.ds(pl.multiple_of(page * blk, 128), blk), :], rgx.at[page], gs.at[page], gr.at[page], x_peer)
 
     def input_grads(page):
         here = pl.ds(pl.multiple_of(page * own, own), own)
-        total = g1_v[page]
-        for grad, w in ((dq_all, gq_v), (dk_all, gk_v), (dv_all, gv_v)):
-            total = total + dot(grad[here, :], w[...], NT)
-        gx[pages * x + page] = total[:blk]
-        gxs[page] = total[blk:].astype(BF)
+        total = accs[here, :]
+        for grad, start in ((dq_all, at_gq), (dk_all, at_gk), (dv_all, at_gv)):
+            total = total + dot(grad[here, :], pool[pl.ds(start, d), :], NT)
+        accs[here, :] = total
+        go[pl.ds(pl.multiple_of(page * blk, 128), blk), :] = total[blk:].astype(BF)
         gx_send(page).start()
+        gx_store(page, 0).start()
+
+    def gx_store(page, side):
+        src = accs.at[pl.ds(pl.multiple_of(page * own + side * blk, 128), blk), :]
+        return pltpu.make_async_copy(src, gx.at[pages * (x if side == 0 else 1 - x) + page], os.at[page, side])
 
     n_it = GROUPS * pages
 
     def unit(it, carry):
         for half in range(2):
+
+            if half == 0:
+
+                @pl.when(jnp.logical_and(it >= pages, it < n_it))
+                def _():
+                    for copy in kv_send(it - pages):
+                        copy.wait_send()
 
             @pl.when(it < n_it)
             def _():
@@ -1279,13 +1350,7 @@
                     for copy in kv_send(it):
                         copy.start()
 
-            tick(2 * it + half)
-
-        @pl.when(it == 0)
-        def _():
-            for copy in loads[5:]:
-                copy.wait()
-            x_t[...] = x_v[...].reshape(pages * own, d).T
+            tick(before + 2 * it + half)
 
         @pl.when(jnp.logical_and(it > 0, jnp.logical_and(lax.rem(it, pages) == 0, it <= n_it)))
         def _():
@@ -1308,7 +1373,7 @@
 
     def small_pack():
         for i in range(8):
-            row = brow[0:1, :] if i == 0 else brow[2:3, :] if i == 1 else gvf[i : i + 1, :]
+            row = brow[0:1, :] if i == 0 else brow[2:3, :] if i == 1 else gvs[i : i + 1, :]
             for j in range(8):
                 pack[j, i : i + 1, :ROW] = row[:, ROW * j : ROW * (j + 1)]
         for j in range(8):
@@ -1336,10 +1401,11 @@
             pl.when(it == when)(run)
         return carry
 
-    lax.fori_loop(0, (last + 1) // 2, all_steps, 0)
+    lax.fori_loop(0, (last - before + 2) // 2, all_steps, 0)
     for page in range(pages):
         gx_send(page).wait_recv()
-        gx[pages * (1 - x) + page] = rgx[page].astype(F32)
+        accs[page * own + blk : (page + 1) * own, :] = rgx[page].astype(F32)
+        gx_store(page, 1).start()
     vec_c().wait_recv()
     ovec[...] = vx[1] + vx[2]
 
@@ -1350,55 +1416,67 @@
     lax.fori_loop(0, REST, finish, 0)
     for g in range(GROUPS):
         gstep(g, "drain")
-    for it in range(n_it):
+    for p in range(6, REST):
+        any_first(p).wait_send()
+    for it in range(n_it - pages, n_it):
         for copy in kv_send(it):
             copy.wait_send()
     for page in range(pages):
         gx_send(page).wait_send()
+        gx_store(page, 0).wait()
+        gx_store(page, 1).wait()
     for k in range(7):
         vec_send(k).wait_send()
+    back_out.wait()
+    stay_out.wait()
     vec_x().wait_send()
     vec_c().wait_send()
 
 
-def bwd(q, k, v, ctx, dctx, gm1, xall, ws, p, grads, gvf, gbin, shards):
-    pages, own, d = q.shape
-    rows, blk = k.shape[1], own // 2
+def bwd(kept, shards):
+    (gq, gk, gv, xall, q, k, v, ctx, p, go, gi, g2, act, dd, hid, gout, n1, gm2, r1, out, gvs, vec) = kept
+    pages, own, d = ctx.shape
+    rows, blk = 2 * own, own // 2
     n = pages * own
     dma = pltpu.SemaphoreType.DMA
     vm = pltpu.VMEM
     sds = jax.ShapeDtypeStruct
-    dwo, dwi, dw2 = grads
-    views = [dwo.reshape(4, 2, ROW, d), dwi.reshape(-1, 4, 2, ROW, d), dw2.reshape((4, 2) + shards[5])]
+    n_chunks = act.shape[0]
+    flat = lambda a: a.reshape(-1, d)
+    args = (
+        flat(gq), flat(gk), flat(gv), xall, flat(q), flat(k), flat(v), ctx, p, flat(go),
+        gi.reshape(n_chunks, d, d), g2.reshape(n_chunks, d, d), act, dd, hid, gout, n1, gm2, r1, out, gvs, vec,
+    )
     res = call(
         bwd_body,
-        (12 * n * d * d + pages * 10 * own * rows * d, sum(16 * g.size for g in grads), 0),
-        in_specs=[ANY] * 14 + [VM, VM],
-        out_specs=[VM] * 8,
+        (24 * n * d * d + pages * 10 * own * rows * d, 60 << 20, 0),
+        in_specs=[ANY] * 20 + [VM, VM],
+        out_specs=[VM] * 6 + [ANY, ANY, VM],
         out_shape=[sds(shape, F32) for shape in shards]
-        + [sds((2 * pages, blk, d), F32), sds((16, 128), F32)],
+        + [sds((2 * pages, blk, d), F32), sds((2 * pages, blk, d), BF), sds((16, 128), F32)],
         scratch_shapes=[
-            vm((pages, own, d), BF), vm((pages, rows, d), BF), vm((pages, rows, d), BF),
-            vm((pages, own, d), BF), vm((pages, own, d), BF), vm((pages, own, d), F32), vm((pages, own, d), BF),
-            vm((d, d), BF), vm((d, d), BF), vm((d, d), BF),
-            vm((REST, 4, 2, ROW, 384), BF), vm((GROUPS, 3, 4, 2, ROW, GCOLS), BF),
+            vm((8 * n, d), BF), vm((n, d), BF), vm((n, d), BF), vm((d, d), BF), vm((n, d), BF), vm((n, d), F32),
+            vm((n, 128), F32), vm((pages, own, d), BF), vm((pages, own, d), BF),
+            vm((REST, 4, 2, ROW, 384), BF), vm((GROUPS, 4, 2, ROW, 3 * GCOLS), BF), vm((3, 4, 2, ROW, 384), BF),
             vm((n, d), BF), vm((n, d), BF), vm((n, d), BF),
-            vm((pages, own, d), BF), vm((pages, own, d), BF), vm((pages, own, d), BF), vm((pages, own, d), BF),
-            vm((2, 2, rows, own), BF), vm((d, n), BF), vm((pages, blk, d), BF), vm((pages, blk, d), BF),
+            vm((pages, own, d), BF), vm((pages, own, d), BF), vm((pages, own, GCOLS), BF), vm((pages, own, GCOLS), BF),
+            vm((2, 2, rows, own), BF), vm((pages, blk, d), BF),
             vm((8, 16, 128), F32), vm((7, 16, 128), F32), vm((16, 128), F32), vm((3, 16, 128), F32), vm((8, d), F32),
+            vm((8, d), F32), vm((1, n_chunks * d), F32), vm((pages, blk, d), BF),
         ]
         + fold_bufs(384, KEEP_REST, REST)
         + fold_bufs(128, KEEP_GROUP, GROUPS, 3)
         + fold_sems(REST)
         + fold_sems(GROUPS, 3)
         + [
-            dma((10,)), dma((REST,)), dma((2,)), dma((GROUPS, pages, 2)), dma((GROUPS, pages, 2)),
-            dma((pages,)), dma((pages,)), dma((7,)), dma((7,)), dma((2,)), dma((2,)),
+            dma((7,)), dma((4, 2)), dma((6 + pages,)), dma((2,)), dma((GROUPS, pages, 2)), dma((GROUPS, pages, 2)),
+            dma((pages,)), dma((pages,)), dma((pages, 2)), dma((7,)), dma((7,)), dma((2,)), dma((2,)),
+            dma((1,)), dma((1,)), dma((2,)),
         ],
         params=dict(collective_id=1, has_side_effects=True, vmem_limit_bytes=64 << 20),
-        name="attention_reduce",
-    )(q, k, v, ctx, dctx, gm1, xall, *ws, p, *views, gvf, gbin)
-    return res[:6], res[6], res[7]
+        name="backward_reduce",
+    )(*args)
+    return res[:6], res[6], res[7], res[8]
 
 
 def finish_body(*refs):
@@ -1464,8 +1542,7 @@
     order = jnp.stack([s, s ^ 2, s ^ 1, s ^ 3]).astype(jnp.int32)
     thr = pages_of(lengths, x_at).astype(jnp.int32)[:, None] - order[None, :] * blk
     if direct:
-        full, rest = fwd(lengths.astype(jnp.int32), inputs, cotangent, ws, names + (b_inner,))
-        xall, q, k, v, ctx, p, dctx, gm1, dwo, dwi, dw2, output, gv_ffn, gbin = rest
+        kept = fwd(lengths.astype(jnp.int32), inputs, cotangent, ws, names + (b_inner,))
     else:
         wq, wk, wv, wo, wi, w2 = [lax.all_gather(w, "fsdp", axis=0, tiled=True) for w in ws]
         vec = jnp.concatenate(names + (b_inner,)).reshape(12, width)
@@ -1481,9 +1558,7 @@
         xall = jnp.concatenate([xown, swap(xown, SWAP_C)], axis=1)
         q, k, v, p, ctx = attn_fwd(thr, xall, wq, wk, wv, vec_full)
     if direct:
-        tot, grad_inputs, tvec = bwd(
-            q, k, v, ctx, dctx, gm1.reshape(pages, 2 * blk, d), xall, full, p, (dwo, dwi, dw2), gv_ffn, gbin, shards
-        )
+        tot, grad_inputs, output, tvec = bwd(kept, shards)
         res = finish((output, grad_inputs) + tuple(tot), tvec, width, b_inner.shape[0])
         output, grad_inputs, tot, small, g_bi = res[0], res[1], res[2:8], res[8:16], res[16]
     else:

time: 217 us -> 210 us (0.968)
  Pallas kernels: 216 us -> 209 us
    pallas_call x1, Pallas kernels: 114 us -> 96.2 us  [fwd(): call(fwd_body, (n * d * (12 * ff + 12 * d), sum((16 * w.size for w in ws)...]
    pallas_call x1, Pallas kernels: 94.5 us -> 105 us  [bwd(): call(bwd_body, (24 * n * d * d + pages * 10 * own * rows * d, 60 << 20, 0...]
where the time goes in v2:
time: 210 us; the launch traced here: 209 us
  Pallas kernels  209 us (100%)
    pallas_call x1, Pallas kernels, bwd(): call(bwd_body, (24 * n * d * d + pages * 10 * own * rows * d, 60 << 20, 0...  105 us
    pallas_call x1, Pallas kernels, fwd(): call(fwd_body, (n * d * (12 * ff + 12 * d), sum((16 * w.size for w in ws)...  96.2 us
    pallas_call x1, Pallas kernels, finish(): call(finish_body, (0, 2 * sum((a.size * a.dtype.itemsize for a in arrays)...  7.11 us

profile of v2, /device:TPU:0, one launch (start us, length us, event | category | flops | bytes accessed | tf_op | source)
XLA Modules:
  0.0 209.4 jit_solution(9149355076806644906)
XLA Ops:
  0.7 96.2 %gather_forward.1 = (bf16[4,2,96,768]{3,2,1,0:T(8,128)(2,1)}, bf16[4,2,96,768]{3,2,1,0:T(8,128)(2,1)}, bf16[4,2,96,768]{3,2,1,0:T(8,128)(2,1)}, bf16[3,512,768]{...) custom-call(s32[6]{0:T(128)} %lens.1, ...), custom_call_target="tpu_custom_call" | custom-call | flops 27179089920 | bytes 14155776 | tf_op jit(solution)/shard_map/gather_forward/pallas_call | solution.py:824
  96.9 105.2 %backward_reduce.1 = (f32[96,768]{1,0:T(8,128)}, f32[96,768]{1,0:T(8,128)}, f32[96,768]{1,0:T(8,128)}, f32[96,768]{1,0:T(8,128)}, f32[96,3072]{1,0:T(8,128)}, /*...) custom-call(bf16[768,768]{1,0:T(8,128)(2,1)} %bitcast.13, ...), custom_call_target="tpu_custom_call" | custom-call | flops 13891534848 | bytes 62914560 | tf_op jit(solution)/shard_map/backward_reduce/pallas_call | solution.py:1450
  202.1 7.1 %finish.1 = (bf16[6,128,768]{2,1,0:T(8,128)(2,1)}, f32[6,128,768]{2,1,0:T(8,128)}, f32[96,768]{1,0:T(8,128)}, f32[96,768]{1,0:T(8,128)}, f32[96,768]{1,0:T(8,128...) custom-call(bf16[6,128,768]{2,1,0:T(8,128)(2,1)} %get-tuple-element., ...), custom_call_target="tpu_custom_call" | custom-call | bytes 14155776 | tf_op jit(solution)/shard_map/finish/pallas_call | solution.py:1506

commit v3 on v2

--- a/solution.py
+++ b/solution.py
@@ -859,6 +859,7 @@
         self.z, self.y, self.x, self.c = where
         self.acc, self.key = acc, key
         give = ROW - keep
+        self.split = give > 0
         self.rc, self.rx, self.ry, self.rz, self.fin, self.rf = [b.at[key] for b in bufs]
         self.cs, self.cr, self.xs, self.xr, self.ys, self.yr, self.zs, self.zr, self.fs, self.fr, self.es, self.er = sems
         z = self.z
@@ -912,9 +913,14 @@
         first.wait_recv()
         whole = self.part(ALL, ALL, ALL)
         whole[...] = whole[...] + self.rc[...]
-        self.xcopy().start()
+        if self.split:
+            self.xcopy().start()
+        else:
+            self.ycopy().start()
 
     def over_y(self):
+        if not self.split:
+            return
         self.xcopy().wait_recv()
         rows = self.part(ALL, 1 - self.y, self.gain)
         rows[...] = rows[...] + self.rx[...]
@@ -971,7 +977,8 @@
 
     def drain(self, view):
         self.ecopy(view).wait_recv()
-        self.xcopy().wait_send()
+        if self.split:
+            self.xcopy().wait_send()
         self.ycopy().wait_send()
         self.a().wait_send()
         self.b().wait_send()
@@ -990,7 +997,7 @@
 
 ALL = slice(None)
 KEEP_REST = 64
-KEEP_GROUP = 80
+KEEP_GROUP = 96
 
 
 def fold_sems(*lead):
@@ -1002,7 +1009,7 @@
     return [
         pltpu.VMEM(lead + shape, BF)
         for shape in (
-            (4, 2, ROW, width), (4, ROW - keep, width), (4, keep, width), (4, ROW, width), (ROW, width), (ROW, width),
+            (4, 2, ROW, width), (4, max(ROW - keep, 16), width), (4, keep, width), (4, ROW, width), (ROW, width), (ROW, width),
         )
     ]
 
@@ -1098,7 +1105,7 @@
             else:
                 getattr(gfold(g, w), name)()
 
-    stages = (("over_x", 0), ("over_y", 4), ("over_z", 10), ("inside", 15), ("total", 19), ("write", 24))
+    stages = (("over_x", 0), ("over_y", 4), ("over_z", 9), ("inside", 14), ("total", 18), ("write", 22))
     pace = 3
     last = pace * (REST + GROUPS - 1) + stages[-1][1] + 1
 
@@ -1153,11 +1160,10 @@
     stay_in = pltpu.make_async_copy(out_h.at[:, pl.ds(0, blk), :], stay, bl.at[0])
     stay_out = pltpu.make_async_copy(stay, fin_out.at[pages_mine], bl.at[1])
     back_out.start()
-    for copy in firsts[:1]:
+    begin_with = chunk_loads(0)
+    for copy in firsts[:1] + [begin_with[1], begin_with[3]] + firsts[1:2] + [begin_with[0]] + firsts[2:3] + [begin_with[2]]:
         copy.start()
-    for copy in chunk_loads(0):
-        copy.start()
-    for copy in firsts[1:]:
+    for copy in firsts[3:]:
         copy.start()
     for copy in chunk_loads(1):
         copy.start()
@@ -1172,20 +1178,36 @@
 
     n_chunks = gi_h.shape[0]
     firsts[0].wait()
-    firsts[1].wait()
-    firsts[2].wait()
 
     def down(j, carry):
-        for copy in chunk_loads(j):
-            copy.wait()
+        wi_in, w2_in, act_in, dd_in = chunk_loads(j)
+        w2_in.wait()
+        dd_in.wait()
         cols = pl.ds(pl.multiple_of(j * d, d), d)
         di = (dot(gout[...], slot(1, j)[...], NT) * slot(3, j)[...].astype(F32)).astype(BF)
-        accs[...] += dot(di, slot(0, j)[...], NT)
-        gbin[:, cols] = jnp.sum(di.astype(F32), 0, keepdims=True)
+
+        @pl.when(j == 0)
+        def _():
+            firsts[1].wait()
+
         keep, pass_on = halves(dot(hid[...], di, TN).astype(BF))
         acc[j] = keep.reshape(4, 2, ROW, 384)
         other_half(j, lambda ref: ref.__setitem__(Ellipsis, pass_on.reshape(4, 2, ROW, 384)))
         launch(j)
+
+        @pl.when(j == 0)
+        def _():
+            firsts[2].wait()
+
+        @pl.when(j > 0)
+        def _():
+            tick(pace * j - 2)
+            tick(pace * j - 1)
+
+        wi_in.wait()
+        accs[...] += dot(di, slot(0, j)[...], NT)
+        gbin[:, cols] = jnp.sum(di.astype(F32), 0, keepdims=True)
+        act_in.wait()
         keep, pass_on = halves(dot(slot(2, j)[...], gout[...], TN).astype(BF))
         keep, pass_on = keep.reshape(2, 4, ROW, 384), pass_on.reshape(2, 4, ROW, 384)
         for p in range(4):
@@ -1200,10 +1222,7 @@
             for copy in chunk_loads(j + 2):
                 copy.start()
 
-        @pl.when(j > 0)
-        def _():
-            lax.fori_loop(pace * (j - 1), pace * j, lambda t, carry: (tick(t), carry)[1], 0)
-
+        tick(pace * j)
         return carry
 
     lax.fori_loop(0, n_chunks, down, 0)
@@ -1219,7 +1238,7 @@
     def add(row, value):
         gvs[row : row + 1, :] += jnp.sum(value, 0, keepdims=True)
 
-    before = pace * (n_chunks - 1)
+    before = pace * (n_chunks - 1) + 1
     for page in range(pages):
         r = slice(page * own, (page + 1) * own)
         gh = accs[r, :]
@@ -1330,6 +1349,10 @@
     n_it = GROUPS * pages
 
     def unit(it, carry):
+        @pl.when(it == n_it)
+        def _():
+            group_grads(GROUPS - 1)
+
         for half in range(2):
 
             if half == 0:
@@ -1352,7 +1375,7 @@
 
             tick(before + 2 * it + half)
 
-        @pl.when(jnp.logical_and(it > 0, jnp.logical_and(lax.rem(it, pages) == 0, it <= n_it)))
+        @pl.when(jnp.logical_and(it > 0, jnp.logical_and(lax.rem(it, pages) == 0, it < n_it)))
         def _():
             group_grads(lax.div(it, pages) - 1)
 

time: 210 us -> 209 us (level)
  no operation moved by 1% of the time
where the time goes in v3:
time: 209 us; the launch traced here: 208 us
  Pallas kernels  208 us (100%)
    pallas_call x1, Pallas kernels, bwd(): call(bwd_body, (24 * n * d * d + pages * 10 * own * rows * d, 60 << 20, 0...  104 us
    pallas_call x1, Pallas kernels, fwd(): call(fwd_body, (n * d * (12 * ff + 12 * d), sum((16 * w.size for w in ws)...  96.2 us
    pallas_call x1, Pallas kernels, finish(): call(finish_body, (0, 2 * sum((a.size * a.dtype.itemsize for a in arrays)...  7.11 us

profile of v3, /device:TPU:0, one launch (start us, length us, event | category | flops | bytes accessed | tf_op | source)
XLA Modules:
  0.0 208.5 jit_solution(2178964770917163339)
XLA Ops:
  0.7 96.2 %gather_forward.1 = (bf16[4,2,96,768]{3,2,1,0:T(8,128)(2,1)}, bf16[4,2,96,768]{3,2,1,0:T(8,128)(2,1)}, bf16[4,2,96,768]{3,2,1,0:T(8,128)(2,1)}, bf16[3,512,768]{...) custom-call(s32[6]{0:T(128)} %lens.1, ...), custom_call_target="tpu_custom_call" | custom-call | flops 27179089920 | bytes 14155776 | tf_op jit(solution)/shard_map/gather_forward/pallas_call | solution.py:824
  96.9 104.3 %backward_reduce.1 = (f32[96,768]{1,0:T(8,128)}, f32[96,768]{1,0:T(8,128)}, f32[96,768]{1,0:T(8,128)}, f32[96,768]{1,0:T(8,128)}, f32[96,3072]{1,0:T(8,128)}, /*...) custom-call(bf16[768,768]{1,0:T(8,128)(2,1)} %bitcast.13, ...), custom_call_target="tpu_custom_call" | custom-call | flops 13891534848 | bytes 62914560 | tf_op jit(solution)/shard_map/backward_reduce/pallas_call | solution.py:1473
  201.2 7.1 %finish.1 = (bf16[6,128,768]{2,1,0:T(8,128)(2,1)}, f32[6,128,768]{2,1,0:T(8,128)}, f32[96,768]{1,0:T(8,128)}, f32[96,768]{1,0:T(8,128)}, f32[96,768]{1,0:T(8,128...) custom-call(bf16[6,128,768]{2,1,0:T(8,128)(2,1)} %get-tuple-element., ...), custom_call_target="tpu_custom_call" | custom-call | bytes 14155776 | tf_op jit(solution)/shard_map/finish/pallas_call | solution.py:1529

commit v4 on v3

--- a/solution.py
+++ b/solution.py
@@ -513,7 +513,7 @@
 GROUPS = 3
 GCOLS = 256
 REST = 9
-EARLY = 3
+EARLY = 2
 YROWS = 64
 
 

time: 209 us -> 207 us (level)
  no operation moved by 1% of the time
where the time goes in v4:
time: 207 us
  Pallas kernels  206 us (100%)
    pallas_call x1, Pallas kernels, bwd(): call(bwd_body, (24 * n * d * d + pages * 10 * own * rows * d, 60 << 20, 0...  103 us
    pallas_call x1, Pallas kernels, fwd(): call(fwd_body, (n * d * (12 * ff + 12 * d), sum((16 * w.size for w in ws)...  96.3 us
    pallas_call x1, Pallas kernels, finish(): call(finish_body, (0, 2 * sum((a.size * a.dtype.itemsize for a in arrays)...  7.11 us

profile of v4, /device:TPU:0, one launch (start us, length us, event | category | flops | bytes accessed | tf_op | source)
XLA Modules:
  0.0 206.8 jit_solution(990363912708109528)
XLA Ops:
  0.7 96.3 %gather_forward.1 = (bf16[4,2,96,768]{3,2,1,0:T(8,128)(2,1)}, bf16[4,2,96,768]{3,2,1,0:T(8,128)(2,1)}, bf16[4,2,96,768]{3,2,1,0:T(8,128)(2,1)}, bf16[3,512,768]{...) custom-call(s32[6]{0:T(128)} %lens.1, ...), custom_call_target="tpu_custom_call" | custom-call | flops 27179089920 | bytes 14155776 | tf_op jit(solution)/shard_map/gather_forward/pallas_call | solution.py:824
  97.0 102.5 %backward_reduce.1 = (f32[96,768]{1,0:T(8,128)}, f32[96,768]{1,0:T(8,128)}, f32[96,768]{1,0:T(8,128)}, f32[96,768]{1,0:T(8,128)}, f32[96,3072]{1,0:T(8,128)}, /*...) custom-call(bf16[768,768]{1,0:T(8,128)(2,1)} %bitcast.13, ...), custom_call_target="tpu_custom_call" | custom-call | flops 13891534848 | bytes 62914560 | tf_op jit(solution)/shard_map/backward_reduce/pallas_call | solution.py:1473
  199.5 7.1 %finish.1 = (bf16[6,128,768]{2,1,0:T(8,128)(2,1)}, f32[6,128,768]{2,1,0:T(8,128)}, f32[96,768]{1,0:T(8,128)}, f32[96,768]{1,0:T(8,128)}, f32[96,768]{1,0:T(8,128...) custom-call(bf16[6,128,768]{2,1,0:T(8,128)(2,1)} %get-tuple-element., ...), custom_call_target="tpu_custom_call" | custom-call | bytes 14155776 | tf_op jit(solution)/shard_map/finish/pallas_call | solution.py:1529
